TPU v7x, 128 devices: a whole 4x4x4 slice. The times are simulated.
128 devices in a mesh: expert: 16 (over z, y), group: 8 (over x, core).
Axes of the slice: x: 4, y: 4, z: 4, core: 2. Of those that a mesh axis runs over, the one named last changes fastest.
Arguments:
- tokens: bfloat16 [2, 16384, 2048], P(None, ('expert', 'group')), may hold values from -6 to 6
- expert_ids: int32 [2, 16384, 8], P(None, ('expert', 'group')), may hold values from 0 to 127, all different within a row; in each aligned block of 128 rows (0 to 127, 128 to 255, ..., all dimensions but the last counted through in order) at most 10 rows name the same one
- gate_probs: float32 [2, 16384, 8], P(None, ('expert', 'group')), may hold values from 0.05 to 1
- capacity: int32 [128], P(('expert', 'group')), may hold values from 448 to 896, as said below
- flows: int32 [128, 3], P(('expert', 'group')), may hold values from 0 to 64, as said below
- w_gate: bfloat16 [128, 2048, 768], P(('expert', 'group')), may hold values from -0.125 to 0.125
- w_up: bfloat16 [128, 2048, 768], P(('expert', 'group')), may hold values from -0.125 to 0.125
- w_down: bfloat16 [128, 768, 2048], P(('expert', 'group')), may hold values from -0.21875 to 0.21875
Outputs:
- mixed: bfloat16 [2, 16384, 2048], P(None, ('expert', 'group'))
Inputs may be any that keep to these rules, and one draw needn't show every extreme that they name: `expert_ids`: among one device's 128 tokens of a micro-batch no expert is chosen more than 10 times, a bound that some block reaches; a token never chooses an expert twice. Some expert has capacity exactly 896. `flows`: some expert has all its grants exactly 64, the same expert that has capacity 896.
All inputs are finite; a program needn't handle non-finite values.
Results may differ from a plain program's by a relative error of at most 0.0085.
Values may be sent and summed in bfloat16 or wider, within the bound.
No kernel may reach another device: no remote copies, remote signals or barrier semaphores. Data moves between devices by JAX's collectives and lax.ppermute only.
A program may use at most 128 MiB of HBM per device.

v0:
```python
import jax
import jax.numpy as jnp
from jax import lax
from jax.sharding import PartitionSpec as P


def split_up(x, dim, devices):
    shape = x.shape
    parts = x.reshape(*shape[:dim], devices, shape[dim] // devices, *shape[dim + 1 :])
    return jnp.moveaxis(parts, dim, 0)


def in_order(parts, dim):
    parts = jnp.moveaxis(parts, 0, dim)
    shape = parts.shape
    return parts.reshape(*shape[:dim], shape[dim] * shape[dim + 1], *shape[dim + 2 :])


def one_exchange(x, axis, axes, splits, concats):
    sizes = [lax.axis_size(a) for a in axes]
    parts = split_up(x, splits[0], sizes[0])
    parts = jnp.moveaxis(split_up(parts, splits[1] + 1, sizes[1]), 0, 1)
    inside = parts.shape[2:]
    parts = parts.reshape(-1, *inside)
    parts = lax.all_to_all(parts, axis, split_axis=0, concat_axis=0, tiled=True)
    parts = in_order(parts.reshape(*sizes, *inside), concats[0] + 1)
    return in_order(parts, concats[1])


def swiglu_rows(rows_in, gate_mat, up_mat, down_mat):
    gate_val = jnp.dot(rows_in, gate_mat, preferred_element_type=jnp.float32)
    up_val = jnp.dot(rows_in, up_mat, preferred_element_type=jnp.float32)
    hidden = (jax.nn.silu(gate_val) * up_val).astype(jnp.bfloat16)
    return jnp.dot(hidden, down_mat, preferred_element_type=jnp.float32).astype(jnp.bfloat16)


def body(tokens, expert_ids, gate_probs, capacity, flows, w_gate, w_up, w_down):
    device_count = lax.axis_size(("expert", "group"))
    expert_count = lax.axis_size("expert")
    group_count = lax.axis_size("group")
    micro_count, tok_local, model_dim = tokens.shape
    top_count = expert_ids.shape[2]
    slot_count = tok_local * top_count * 5 // (4 * device_count)
    slot_total = device_count * slot_count
    keep_limit = capacity[0] + jnp.sum(flows[0])
    expert_iota = jnp.arange(device_count, dtype=jnp.int32)
    slot_all = jnp.arange(slot_total, dtype=jnp.int32)
    slot_iota = jnp.arange(slot_count, dtype=jnp.int32)
    zero_row = jnp.zeros((), jnp.bfloat16)
    results = []
    for micro_index in range(micro_count):
        local_rows = tokens[micro_index]
        pair_expert = expert_ids[micro_index].reshape(-1)
        onehot = (pair_expert[:, None] == expert_iota[None, :]).astype(jnp.int32)
        slot_rank = jnp.sum((jnp.cumsum(onehot, 0) - onehot) * onehot, 1)
        counts = jnp.sum(onehot, 0)
        flat_slot = pair_expert * slot_count + slot_rank
        matches = (flat_slot[:, None] == slot_all[None, :]).reshape(
            tok_local, top_count, slot_total
        )
        select = jnp.any(matches, 1).astype(jnp.bfloat16)
        outgoing = lax.dot_general(
            select, local_rows, (((0,), (0,)), ((), ())), preferred_element_type=jnp.float32
        ).astype(jnp.bfloat16)
        outgoing = outgoing.reshape(device_count, slot_count, model_dim)
        sectioned_rows, sectioned_counts = (
            one_exchange(
                outgoing.reshape(expert_count, group_count, slot_count, model_dim),
                ("expert", "group"),
                ("expert", "group"),
                (0, 1),
                (0, 1),
            ),
            one_exchange(
                counts.reshape(expert_count, group_count),
                ("expert", "group"),
                ("expert", "group"),
                (0, 1),
                (0, 1),
            ),
        )
        incoming = sectioned_rows.reshape(device_count, slot_count, model_dim)
        arrived_counts = sectioned_counts.reshape(device_count)
        offset = jnp.cumsum(arrived_counts) - arrived_counts
        back_pos = offset[:, None] + slot_iota[None, :]
        back_live = (slot_iota[None, :] < arrived_counts[:, None]) & (back_pos < keep_limit)
        expert_out = swiglu_rows(
            incoming.reshape(slot_total, model_dim), w_gate[0], w_up[0], w_down[0]
        )
        returned = jnp.where(back_live.reshape(-1)[:, None], expert_out, zero_row)
        returned = returned.reshape(device_count, slot_count, model_dim)
        answered = one_exchange(
            returned.reshape(expert_count, group_count, slot_count, model_dim),
            ("expert", "group"),
            ("expert", "group"),
            (0, 1),
            (0, 1),
        )
        answered = answered.reshape(slot_total, model_dim)
        probs = gate_probs[micro_index]
        gate_norm = probs / jnp.sum(probs, 1, keepdims=True)
        weights = jnp.sum(matches.astype(jnp.float32) * gate_norm[:, :, None], 1)
        weight_high = weights.astype(jnp.bfloat16)
        weight_low = (weights - weight_high.astype(jnp.float32)).astype(jnp.bfloat16)
        mixed = jnp.dot(weight_high, answered, preferred_element_type=jnp.float32)
        mixed = mixed + jnp.dot(weight_low, answered, preferred_element_type=jnp.float32)
        results.append(mixed.astype(jnp.bfloat16))
    return jnp.stack(results)


def solution(mesh):
    placed = (
        P(None, ("expert", "group"), None),
        P(None, ("expert", "group"), None),
        P(None, ("expert", "group"), None),
        P(("expert", "group")),
        P(("expert", "group"), None),
        P(("expert", "group"), None, None),
        P(("expert", "group"), None, None),
        P(("expert", "group"), None, None),
    )
    return jax.shard_map(
        body,
        mesh=mesh,
        in_specs=placed,
        out_specs=P(None, ("expert", "group"), None),
        check_vma=False,
    )
```

profile of v0, /device:TPU:90, one launch (start us, length us, event | category | flops | bytes accessed | tf_op | source)
XLA Modules:
  0.0 508.1 jit_solution(15896305224433901497)
XLA Ops:
  4.6 10.3 %all-to-all-start.3 = ((s32[128,1,1]{2,1,0:T(1,128)}), s32[128,1,1]{2,1,0:T(1,128)}, u32[]{:S(2)}, u32[]{:S(2)}) async-start(s32[128,1,1]{2,1,0:T(1,128)} %copy.74), calls=%async_computation.3 | async-start | bytes 131072 | tf_op jit(solution)/shard_map/all_to_all | solution.py:25
  20.4 9.8 %all-to-all-start = ((s32[128,1,1]{2,1,0:T(1,128)}), s32[128,1,1]{2,1,0:T(1,128)S(1)}, u32[]{:S(2)}, u32[]{:S(2)}) async-start(s32[128,1,1]{2,1,0:T(1,128)} %copy.63), calls=%async_computation | async-start | bytes 131072 | tf_op jit(solution)/shard_map/all_to_all | solution.py:25
  30.2 5.0 convolution_convert_fusion.1
  35.2 9.5 %reshape_transpose_transpose_reshape_reshape_reshape_reshape.14 = bf16[128,1,1,10,2048]{4,3,0,2,1:T(8,128)(2,1)} reshape(bf16[1280,2048]{1,0:T(8,128)(2,1)} %convolution_convert_fusion.1) | data formatting | bytes 10485760 | tf_op jit(solution)/shard_map/reshape;transpose;transpose;reshape;reshape;reshape;reshape | solution.py:24
  44.7 10.2 %all-to-all-start.4 = ((bf16[128,1,1,10,2048]{4,3,2,1,0:T(8,128)(2,1)}), bf16[128,1,1,10,2048]{4,3,2,1,0:T(8,128)(2,1)}, u32[]{:S(2)}, u32[]{:S(2)}) async-start(bf16[128,1,1,10,2048]{4,3,2,1,0:T(8,128)(2,1)} %bitcast.120), calls=%async_computation.4 | async-start | bytes 16777216 | tf_op jit(solution)/shard_map/all_to_all | solution.py:25
  56.7 5.0 convolution_convert_fusion.3
  61.7 9.5 %reshape_transpose_transpose_reshape_reshape_reshape_reshape.12 = bf16[128,1,1,10,2048]{4,3,0,2,1:T(8,128)(2,1)} reshape(bf16[1280,2048]{1,0:T(8,128)(2,1)} %convolution_convert_fusion.3) | data formatting | bytes 10485760 | tf_op jit(solution)/shard_map/reshape;transpose;transpose;reshape;reshape;reshape;reshape | solution.py:24
  71.2 86.6 %all-to-all-done.4 = bf16[128,1,1,10,2048]{4,3,2,1,0:T(8,128)(2,1)} async-done(((bf16[128,1,1,10,2048]{4,3,2,1,0:T(8,128)(2,1)}), bf16[128,1,1,10,2048]{4,3,2,1,0:T(8,128)(2,1)}, u32[]{:S(2)}, u32[]{:S(2)}) %all-to-all-start.4) | async-done | bytes 5242912 | tf_op jit(solution)/shard_map/all_to_all | solution.py:25
  157.8 9.1 %all-to-all-start.1 = ((bf16[128,1,1,10,2048]{4,3,2,1,0:T(8,128)(2,1)}), bf16[128,1,1,10,2048]{4,3,2,1,0:T(8,128)(2,1)}, u32[]{:S(2)}, u32[]{:S(2)}) async-start(bf16[128,1,1,10,2048]{4,3,2,1,0:T(8,128)(2,1)} %bitcast.117), calls=%async_computation.1 | async-start | bytes 16777216 | tf_op jit(solution)/shard_map/all_to_all | solution.py:25
  168.9 3.2 reduce.5
  173.1 9.9 %reshape_reshape_reshape.7 = bf16[1280,2048]{1,0:T(8,128)(2,1)} reshape(bf16[16,8,1,10,2048]{4,3,1,0,2:T(8,128)(2,1)} %bitcast.41) | data formatting | bytes 10485760 | tf_op jit(solution)/shard_map/reshape;reshape;reshape | solution.py:88
  182.9 7.2 %fusion.10 = f32[1280,768]{1,0:T(8,128)S(1)} fusion(bf16[1280,2048]{1,0:T(8,128)(2,1)} %reshape_reshape_reshape.7, bf16[1,2048,768]{2,1,0:T(8,128)(2,1)} %param.13), kind=kOutput, calls=%fused_computation.20 | convolution fusion | flops 4026531840 | bytes 12320768 | tf_op jit(solution)/shard_map/dot_general | solution.py:31
  190.2 4.8 fusion.5
  195.0 6.0 %fusion.1 = bf16[1280,2048]{1,0:T(8,128)(2,1)} fusion(bf16[1280,768]{1,0:T(8,128)(2,1)S(1)} %fusion.5, pred[1280]{0:T(1024)(128)(4,1)S(1)} %and.23, bf16[1,768,2048]{2,1,0:T(8,128)(2,1)S(1)} %copy-done), kind=kOutput, calls=%fused_computation.5 | convolution fusion | flops 4031774720 | bytes 10355968 | tf_op jit(solution)/shard_map/dot_general | solution.py:34
  201.1 9.5 %reshape_transpose_transpose_reshape_reshape_reshape_reshape.15 = bf16[128,1,1,10,2048]{4,3,0,2,1:T(8,128)(2,1)} reshape(bf16[1280,2048]{1,0:T(8,128)(2,1)} %fusion.1) | data formatting | bytes 10485760 | tf_op jit(solution)/shard_map/reshape;transpose;transpose;reshape;reshape;reshape;reshape | solution.py:24
  210.6 58.7 %all-to-all-done.1 = bf16[128,1,1,10,2048]{4,3,2,1,0:T(8,128)(2,1)} async-done(((bf16[128,1,1,10,2048]{4,3,2,1,0:T(8,128)(2,1)}), bf16[128,1,1,10,2048]{4,3,2,1,0:T(8,128)(2,1)}, u32[]{:S(2)}, u32[]{:S(2)}) %all-to-all-start.1) | async-done | bytes 5242912 | tf_op jit(solution)/shard_map/all_to_all | solution.py:25
  269.3 8.8 %all-to-all-start.5 = ((bf16[128,1,1,10,2048]{4,3,2,1,0:T(8,128)(2,1)}), bf16[128,1,1,10,2048]{4,3,2,1,0:T(8,128)(2,1)}, u32[]{:S(2)}, u32[]{:S(2)}) async-start(bf16[128,1,1,10,2048]{4,3,2,1,0:T(8,128)(2,1)} %bitcast.118), calls=%async_computation.5 | async-start | bytes 16777216 | tf_op jit(solution)/shard_map/all_to_all | solution.py:25
  278.1 2.4 reduce.3
  281.4 9.9 %reshape_reshape_reshape.6 = bf16[1280,2048]{1,0:T(8,128)(2,1)} reshape(bf16[16,8,1,10,2048]{4,3,1,0,2:T(8,128)(2,1)} %bitcast.16) | data formatting | bytes 10485760 | tf_op jit(solution)/shard_map/reshape;reshape;reshape | solution.py:88
  291.3 7.2 %fusion.12 = f32[1280,768]{1,0:T(8,128)S(1)} fusion(bf16[1280,2048]{1,0:T(8,128)(2,1)} %reshape_reshape_reshape.6, bf16[1,2048,768]{2,1,0:T(8,128)(2,1)} %param.13), kind=kOutput, calls=%fused_computation.22 | convolution fusion | flops 4026531840 | bytes 12320768 | tf_op jit(solution)/shard_map/dot_general | solution.py:31
  298.6 4.8 fusion.4
  303.4 6.0 %fusion = bf16[1280,2048]{1,0:T(8,128)(2,1)} fusion(bf16[1280,768]{1,0:T(8,128)(2,1)S(1)} %fusion.4, pred[1280]{0:T(1024)(128)(4,1)S(1)} %and.21, bf16[1,768,2048]{2,1,0:T(8,128)(2,1)S(1)} %copy-done), kind=kOutput, calls=%fused_computation.4 | convolution fusion | flops 4031774720 | bytes 10355968 | tf_op jit(solution)/shard_map/dot_general | solution.py:34
  309.4 9.5 %reshape_transpose_transpose_reshape_reshape_reshape_reshape.13 = bf16[128,1,1,10,2048]{4,3,0,2,1:T(8,128)(2,1)} reshape(bf16[1280,2048]{1,0:T(8,128)(2,1)} %fusion) | data formatting | bytes 10485760 | tf_op jit(solution)/shard_map/reshape;transpose;transpose;reshape;reshape;reshape;reshape | solution.py:24
  319.0 61.5 %all-to-all-done.5 = bf16[128,1,1,10,2048]{4,3,2,1,0:T(8,128)(2,1)} async-done(((bf16[128,1,1,10,2048]{4,3,2,1,0:T(8,128)(2,1)}), bf16[128,1,1,10,2048]{4,3,2,1,0:T(8,128)(2,1)}, u32[]{:S(2)}, u32[]{:S(2)}) %all-to-all-start.5) | async-done | bytes 5242912 | tf_op jit(solution)/shard_map/all_to_all | solution.py:25
  380.4 8.9 %all-to-all-start.2 = ((bf16[128,1,1,10,2048]{4,3,2,1,0:T(8,128)(2,1)}), bf16[128,1,1,10,2048]{4,3,2,1,0:T(8,128)(2,1)}, u32[]{:S(2)}, u32[]{:S(2)}) async-start(bf16[128,1,1,10,2048]{4,3,2,1,0:T(8,128)(2,1)} %bitcast.119), calls=%async_computation.2 | async-start | bytes 16777216 | tf_op jit(solution)/shard_map/all_to_all | solution.py:25
  389.5 2.5 select_reduce_fusion
  392.0 2.5 select_reduce_fusion.1
  394.5 9.8 %reshape_reshape.9 = bf16[1280,2048]{1,0:T(8,128)(2,1)} reshape(bf16[16,8,1,10,2048]{4,3,1,0,2:T(8,128)(2,1)} %bitcast.46) | data formatting | bytes 10485760 | tf_op jit(solution)/shard_map/reshape;reshape | solution.py:99
  404.3 3.7 fusion.33
  410.4 81.2 %all-to-all-done.2 = bf16[128,1,1,10,2048]{4,3,2,1,0:T(8,128)(2,1)} async-done(((bf16[128,1,1,10,2048]{4,3,2,1,0:T(8,128)(2,1)}), bf16[128,1,1,10,2048]{4,3,2,1,0:T(8,128)(2,1)}, u32[]{:S(2)}, u32[]{:S(2)}) %all-to-all-start.2) | async-done | bytes 5242912 | tf_op jit(solution)/shard_map/all_to_all | solution.py:25
  491.6 9.8 %reshape_reshape.8 = bf16[1280,2048]{1,0:T(8,128)(2,1)} reshape(bf16[16,8,1,10,2048]{4,3,1,0,2:T(8,128)(2,1)} %bitcast.24) | data formatting | bytes 10485760 | tf_op jit(solution)/shard_map/reshape;reshape | solution.py:99
  501.4 3.7 fusion.36
  (89 shorter events, 19.6 us)
Async XLA Ops:
  0.0 195.0 %copy-start = (bf16[1,768,2048]{2,1,0:T(8,128)(2,1)S(1)}, bf16[1,768,2048]{2,1,0:T(8,128)(2,1)}, u32[]{:S(2)}) copy-start(bf16[1,768,2048]{2,1,0:T(8,128)(2,1)} %param.15) | copy-start | bytes 9437188
  1.5 0.8 copy-start.7
  4.6 15.8 %all-to-all-start.3 = ((s32[128,1,1]{2,1,0:T(1,128)}), s32[128,1,1]{2,1,0:T(1,128)}, u32[]{:S(2)}, u32[]{:S(2)}) async-start(s32[128,1,1]{2,1,0:T(1,128)} %copy.74), calls=%async_computation.3 | async-start | bytes 131072 | tf_op jit(solution)/shard_map/all_to_all | solution.py:25
  17.3 0.8 copy-start.8
  20.4 24.3 %all-to-all-start = ((s32[128,1,1]{2,1,0:T(1,128)}), s32[128,1,1]{2,1,0:T(1,128)S(1)}, u32[]{:S(2)}, u32[]{:S(2)}) async-start(s32[128,1,1]{2,1,0:T(1,128)} %copy.63), calls=%async_computation | async-start | bytes 131072 | tf_op jit(solution)/shard_map/all_to_all | solution.py:25
  44.7 113.1 %all-to-all-start.4 = ((bf16[128,1,1,10,2048]{4,3,2,1,0:T(8,128)(2,1)}), bf16[128,1,1,10,2048]{4,3,2,1,0:T(8,128)(2,1)}, u32[]{:S(2)}, u32[]{:S(2)}) async-start(bf16[128,1,1,10,2048]{4,3,2,1,0:T(8,128)(2,1)} %bitcast.120), calls=%async_computation.4 | async-start | bytes 16777216 | tf_op jit(solution)/shard_map/all_to_all | solution.py:25
  157.8 9.8 %copy-start.13 = (s32[1,3]{1,0:T(1,128)S(1)}, s32[1,3]{1,0:T(1,128)}, u32[]{:S(2)}) copy-start(s32[1,3]{1,0:T(1,128)} %param.12) | copy-start | bytes 40
  157.8 111.4 %all-to-all-start.1 = ((bf16[128,1,1,10,2048]{4,3,2,1,0:T(8,128)(2,1)}), bf16[128,1,1,10,2048]{4,3,2,1,0:T(8,128)(2,1)}, u32[]{:S(2)}, u32[]{:S(2)}) async-start(bf16[128,1,1,10,2048]{4,3,2,1,0:T(8,128)(2,1)} %bitcast.117), calls=%async_computation.1 | async-start | bytes 16777216 | tf_op jit(solution)/shard_map/all_to_all | solution.py:25
  182.9 7.3 %copy-start.5 = (bf16[1280,2048]{1,0:T(8,128)(2,1)S(1)}, bf16[1280,2048]{1,0:T(8,128)(2,1)}, u32[]{:S(2)}) copy-start(bf16[1280,2048]{1,0:T(8,128)(2,1)} %reshape_reshape_reshape.7) | copy-start | bytes 15728644
  182.9 7.3 %copy-start.11 = (bf16[1,2048,768]{2,1,0:T(8,128)(2,1)S(1)}, bf16[1,2048,768]{2,1,0:T(8,128)(2,1)}, u32[]{:S(2)}) copy-start(bf16[1,2048,768]{2,1,0:T(8,128)(2,1)} %param.14) | copy-start | bytes 9437188
  269.3 111.1 %all-to-all-start.5 = ((bf16[128,1,1,10,2048]{4,3,2,1,0:T(8,128)(2,1)}), bf16[128,1,1,10,2048]{4,3,2,1,0:T(8,128)(2,1)}, u32[]{:S(2)}, u32[]{:S(2)}) async-start(bf16[128,1,1,10,2048]{4,3,2,1,0:T(8,128)(2,1)} %bitcast.118), calls=%async_computation.5 | async-start | bytes 16777216 | tf_op jit(solution)/shard_map/all_to_all | solution.py:25
  291.3 7.3 %copy-start.6 = (bf16[1280,2048]{1,0:T(8,128)(2,1)S(1)}, bf16[1280,2048]{1,0:T(8,128)(2,1)}, u32[]{:S(2)}) copy-start(bf16[1280,2048]{1,0:T(8,128)(2,1)} %reshape_reshape_reshape.6) | copy-start | bytes 15728644
  291.3 7.3 %copy-start.12 = (bf16[1,2048,768]{2,1,0:T(8,128)(2,1)S(1)}, bf16[1,2048,768]{2,1,0:T(8,128)(2,1)}, u32[]{:S(2)}) copy-start(bf16[1,2048,768]{2,1,0:T(8,128)(2,1)} %param.14) | copy-start | bytes 9437188
  380.4 8.9 %copy-start.10 = (f32[2,128,8]{1,2,0:T(8,128)S(1)}, f32[2,128,8]{1,2,0:T(8,128)}, u32[]{:S(2)}) copy-start(f32[2,128,8]{1,2,0:T(8,128)} %param.10) | copy-start | bytes 24580
  380.4 111.2 %all-to-all-start.2 = ((bf16[128,1,1,10,2048]{4,3,2,1,0:T(8,128)(2,1)}), bf16[128,1,1,10,2048]{4,3,2,1,0:T(8,128)(2,1)}, u32[]{:S(2)}, u32[]{:S(2)}) async-start(bf16[128,1,1,10,2048]{4,3,2,1,0:T(8,128)(2,1)} %bitcast.119), calls=%async_computation.2 | async-start | bytes 16777216 | tf_op jit(solution)/shard_map/all_to_all | solution.py:25
  404.3 4.2 copy-start.1
  404.3 4.4 copy-start.4
  501.4 4.2 copy-start.2
  501.4 4.4 copy-start.3
  505.8 1.0 copy-start.9
where the time goes:
time: 518 us; the launch traced here: 508 us
  waiting for transfers between devices  288 us (56%)
  local copies, waits for them, and re-layouts  85.5 us (17%)
  starting transfers between devices  57.2 us (11%)
  matrix products  56.1 us (11%)
  other arithmetic  19.6 us (4%)
    all_to_all x6, waiting for transfers between devices, one_exchange(): parts = lax.all_to_all(parts, axis, split_axis=0, concat_axis=0, tiled=True)  288 us
    all_to_all x6, starting transfers between devices, one_exchange(): parts = lax.all_to_all(parts, axis, split_axis=0, concat_axis=0, tiled=True)  57.2 us
    another operation x6, local copies, waits for them, and re-layouts, one_exchange(): parts = parts.reshape(-1, *inside)  39.6 us
    another operation x2, local copies, waits for them, and re-layouts, body(): incoming.reshape(slot_total, model_dim)  19.7 us
    another operation x2, local copies, waits for them, and re-layouts, body(): answered = answered.reshape(slot_total, model_dim)  19.7 us
    dot_general x2, matrix products, swiglu_rows(): gate_val = jnp.dot(rows_in, gate_mat, preferred_element_type=jnp.float32)  14.5 us
    dot_general x2, matrix products, swiglu_rows(): jnp.dot(hidden, down_mat, preferred_element_type=jnp.float32)  12.1 us
  transfers between devices with their start and end apart: 6, of which 4 were waited for; matrix products, arithmetic and copies ran while one was open for 27% of the time, Pallas kernels for 0%

commit v1 on v0

v1 whole, which is shorter than its diff:
```python
import jax
import jax.numpy as jnp
from jax import lax
from jax.experimental import pallas as pl
from jax.experimental.pallas import tpu as pltpu
from jax.sharding import PartitionSpec as P

AXES = ("expert", "group")
PIECES = 4
MARK = 8.0


def place_of(index, per_device):
    device = jnp.floor((index.astype(jnp.float32) + 0.5) * (1.0 / per_device)).astype(jnp.int32)
    inside = index - device * per_device
    return device, inside // PIECES, inside % PIECES


def ranked(ids, experts):
    tok, top = ids.shape
    lane = lax.broadcasted_iota(jnp.int32, (tok, experts), 1)
    chosen = jnp.zeros((tok, experts), jnp.float32)
    for k in range(top):
        chosen = jnp.where(ids[:, k : k + 1] == lane, 1.0, chosen)
    earlier = lax.broadcasted_iota(jnp.int32, (tok, tok), 0) > lax.broadcasted_iota(jnp.int32, (tok, tok), 1)
    before = jnp.dot(
        jnp.where(earlier, 1.0, 0.0).astype(jnp.bfloat16),
        chosen.astype(jnp.bfloat16),
        preferred_element_type=jnp.float32,
    )
    return chosen * (before + 1.0)


def pack_tokens(tokens, ids, micro, slots, block_devices):
    _, tok, width = tokens.shape
    top = ids.shape[2]
    experts = lax.axis_size(AXES)
    per_device = slots * PIECES
    part = width // PIECES
    rows = block_devices * per_device

    def kernel(ids_ref, tok_ref, out_ref, rank_ref, piece_ref):
        step = pl.program_id(0)

        @pl.when(step == 0)
        def _():
            rank_ref[...] = ranked(ids_ref[0], experts).T.astype(jnp.bfloat16)
            for q in range(PIECES):
                piece_ref[q * tok : (q + 1) * tok, :] = tok_ref[0, :, q * part : (q + 1) * part]

        row = lax.broadcasted_iota(jnp.int32, (rows, experts), 0)
        col = lax.broadcasted_iota(jnp.int32, (rows, experts), 1)
        device, slot, piece = place_of(row, per_device)
        spread = jnp.where(device + step * block_devices == col, 1.0, 0.0).astype(jnp.bfloat16)
        rank = jnp.dot(spread, rank_ref[...], preferred_element_type=jnp.float32)
        hit = jnp.where(rank == (slot + 1).astype(jnp.float32), 1.0, 0.0)
        select = jnp.concatenate(
            [jnp.where(piece == q, hit, 0.0).astype(jnp.bfloat16) for q in range(PIECES)], axis=1
        )
        moved = jnp.dot(select, piece_ref[...], preferred_element_type=jnp.float32)
        filled = jnp.sum(hit, axis=1, keepdims=True)
        mark = jnp.where((filled < 0.5) & (piece == 0) & (col == 0), MARK, 0.0)
        out_ref[:, :experts] = (moved[:, :experts] + mark).astype(jnp.bfloat16)
        out_ref[:, experts:] = moved[:, experts:].astype(jnp.bfloat16)

    return pl.pallas_call(
        kernel,
        grid=(experts // block_devices,),
        in_specs=[
            pl.BlockSpec((1, tok, top), lambda i: (micro, 0, 0)),
            pl.BlockSpec((1, tok, width), lambda i: (micro, 0, 0)),
        ],
        out_specs=pl.BlockSpec((rows, part), lambda i: (i, 0)),
        out_shape=jax.ShapeDtypeStruct((experts * per_device, part), jnp.bfloat16),
        scratch_shapes=[
            pltpu.VMEM((experts, tok), jnp.bfloat16),
            pltpu.VMEM((PIECES * tok, part), jnp.bfloat16),
        ],
        name="pack_tokens",
    )(ids, tokens)


def mix_answers(answered, ids, probs, micro, slots, block_devices, earlier_out):
    micros, tok, top = ids.shape
    experts = lax.axis_size(AXES)
    per_device = slots * PIECES
    part = answered.shape[1]
    width = part * PIECES
    rows = block_devices * per_device
    steps = experts // block_devices

    def kernel(ids_ref, probs_ref, rows_ref, *rest):
        out_ref, rank_ref, gate_ref, sum_ref = rest[-4:]
        step = pl.program_id(0)

        @pl.when(step == 0)
        def _():
            ids_here = ids_ref[0]
            probs_here = probs_ref[0]
            norm = probs_here / jnp.sum(probs_here, axis=1, keepdims=True)
            lane = lax.broadcasted_iota(jnp.int32, (tok, experts), 1)
            gate = jnp.zeros((tok, experts), jnp.float32)
            for k in range(top):
                gate = jnp.where(ids_here[:, k : k + 1] == lane, norm[:, k : k + 1], gate)
            gate_ref[...] = gate.astype(jnp.bfloat16)
            rank_ref[...] = ranked(ids_here, experts).astype(jnp.bfloat16)
            sum_ref[...] = jnp.zeros_like(sum_ref)

        lane = lax.broadcasted_iota(jnp.int32, (experts, rows), 1)
        sub = lax.broadcasted_iota(jnp.int32, (experts, rows), 0)
        device, _, _ = place_of(lane, per_device)
        spread = jnp.where(device + step * block_devices == sub, 1.0, 0.0).astype(jnp.bfloat16)
        rank = jnp.dot(rank_ref[...], spread, preferred_element_type=jnp.float32)
        gate = jnp.dot(gate_ref[...], spread, preferred_element_type=jnp.float32)
        _, slot, piece = place_of(lax.broadcasted_iota(jnp.int32, (tok, rows), 1), per_device)
        weight = jnp.where(rank == (slot + 1).astype(jnp.float32), gate, 0.0)
        weights = jnp.concatenate(
            [jnp.where(piece == q, weight, 0.0).astype(jnp.bfloat16) for q in range(PIECES)], axis=0
        )
        sum_ref[...] += jnp.dot(weights, rows_ref[...], preferred_element_type=jnp.float32)

        @pl.when(step == steps - 1)
        def _():
            for q in range(PIECES):
                out_ref[0, :, q * part : (q + 1) * part] = sum_ref[q * tok : (q + 1) * tok, :].astype(
                    jnp.bfloat16
                )

    in_specs = [
        pl.BlockSpec((1, tok, top), lambda i: (micro, 0, 0)),
        pl.BlockSpec((1, tok, top), lambda i: (micro, 0, 0)),
        pl.BlockSpec((rows, part), lambda i: (i, 0)),
    ]
    operands = [ids, probs, answered]
    aliases = {}
    if earlier_out is not None:
        in_specs.append(pl.BlockSpec(memory_space=pl.ANY))
        operands.append(earlier_out)
        aliases = {3: 0}
    return pl.pallas_call(
        kernel,
        grid=(steps,),
        in_specs=in_specs,
        out_specs=pl.BlockSpec((1, tok, width), lambda i: (micro, 0, 0)),
        out_shape=jax.ShapeDtypeStruct((micros, tok, width), jnp.bfloat16),
        scratch_shapes=[
            pltpu.VMEM((tok, experts), jnp.bfloat16),
            pltpu.VMEM((tok, experts), jnp.bfloat16),
            pltpu.VMEM((PIECES * tok, part), jnp.float32),
        ],
        input_output_aliases=aliases,
        name="mix_answers",
    )(*operands)


def run_expert(arrived, keep_limit, gate_mat, up_mat, down_mat, slots, block_devices):
    packed_rows, part = arrived.shape
    width, hidden_dim = gate_mat.shape[1:]
    turn = 16 * slots
    turns = block_devices * slots // turn
    rows = block_devices * slots
    steps = packed_rows // (rows * PIECES)

    def kernel(limit_ref, in_ref, gate_ref, up_ref, down_ref, out_ref, join_ref, split_ref, rows_ref, seen_ref):
        step = pl.program_id(0)

        @pl.when(step == 0)
        def _():
            seen_ref[...] = jnp.zeros_like(seen_ref)
            for q in range(PIECES):
                row = lax.broadcasted_iota(jnp.int32, (turn, turn * PIECES), 0)
                col = lax.broadcasted_iota(jnp.int32, (turn, turn * PIECES), 1)
                join_ref[q] = jnp.where(col == row * PIECES + q, 1.0, 0.0).astype(jnp.bfloat16)
                row = lax.broadcasted_iota(jnp.int32, (turn * PIECES, turn), 0)
                col = lax.broadcasted_iota(jnp.int32, (turn * PIECES, turn), 1)
                split_ref[q] = jnp.where(row == col * PIECES + q, 1.0, 0.0).astype(jnp.bfloat16)

        for j in range(turns):
            pieces = in_ref[j * turn * PIECES : (j + 1) * turn * PIECES, :]
            for q in range(PIECES):
                rows_ref[j * turn : (j + 1) * turn, q * part : (q + 1) * part] = jnp.dot(
                    join_ref[q], pieces, preferred_element_type=jnp.float32
                ).astype(jnp.bfloat16)
        rows_here = rows_ref[...]
        lanes = seen_ref.shape[1]
        live = jnp.where(
            jnp.broadcast_to(rows_here[:, :1].astype(jnp.float32), (rows, lanes)) < MARK - 1.0, 1.0, 0.0
        )
        above = lax.broadcasted_iota(jnp.int32, (rows, rows), 0) > lax.broadcasted_iota(jnp.int32, (rows, rows), 1)
        rank = seen_ref[...] + jnp.dot(
            jnp.where(above, 1.0, 0.0).astype(jnp.bfloat16),
            live.astype(jnp.bfloat16),
            preferred_element_type=jnp.float32,
        )
        seen_ref[...] += jnp.sum(live, axis=0, keepdims=True)
        limit = limit_ref[0].astype(jnp.float32)
        kept = (live > 0.5) & (rank < limit)
        kept = jnp.where(kept, 1.0, 0.0)[:, :1] > 0.5

        gate_val = jnp.dot(rows_here, gate_ref[0], preferred_element_type=jnp.float32)
        up_val = jnp.dot(rows_here, up_ref[0], preferred_element_type=jnp.float32)
        hidden = (gate_val * lax.logistic(gate_val) * up_val).astype(jnp.bfloat16)
        out_val = jnp.dot(hidden, down_ref[0], preferred_element_type=jnp.float32)
        out_val = jnp.where(kept, out_val, 0.0).astype(jnp.bfloat16)
        for j in range(turns):
            moved = jnp.zeros((turn * PIECES, part), jnp.float32)
            for q in range(PIECES):
                moved = moved + jnp.dot(
                    split_ref[q],
                    out_val[j * turn : (j + 1) * turn, q * part : (q + 1) * part],
                    preferred_element_type=jnp.float32,
                )
            out_ref[j * turn * PIECES : (j + 1) * turn * PIECES, :] = moved.astype(jnp.bfloat16)

    return pl.pallas_call(
        kernel,
        grid=(steps,),
        in_specs=[
            pl.BlockSpec(memory_space=pltpu.SMEM),
            pl.BlockSpec((rows * PIECES, part), lambda i: (i, 0)),
            pl.BlockSpec((1, width, hidden_dim), lambda i: (0, 0, 0)),
            pl.BlockSpec((1, width, hidden_dim), lambda i: (0, 0, 0)),
            pl.BlockSpec((1, hidden_dim, width), lambda i: (0, 0, 0)),
        ],
        out_specs=pl.BlockSpec((rows * PIECES, part), lambda i: (i, 0)),
        out_shape=jax.ShapeDtypeStruct((packed_rows, part), jnp.bfloat16),
        scratch_shapes=[
            pltpu.VMEM((PIECES, turn, turn * PIECES), jnp.bfloat16),
            pltpu.VMEM((PIECES, turn * PIECES, turn), jnp.bfloat16),
            pltpu.VMEM((rows, width), jnp.bfloat16),
            pltpu.VMEM((1, 128), jnp.float32),
        ],
        name="run_expert",
    )(keep_limit, arrived, gate_mat, up_mat, down_mat)


def swap(rows, devices):
    parts = rows.reshape(devices, rows.shape[0] // devices, rows.shape[1])
    return lax.all_to_all(parts, AXES, split_axis=0, concat_axis=0, tiled=True)


def body(tokens, expert_ids, gate_probs, capacity, flows, w_gate, w_up, w_down):
    devices = lax.axis_size(AXES)
    micros, tok, width = tokens.shape
    top = expert_ids.shape[2]
    slots = tok * top * 5 // (4 * devices)
    block_devices = 16
    keep_limit = capacity + jnp.sum(flows, 1)

    arrived = []
    for m in range(micros):
        packed = pack_tokens(tokens, expert_ids, m, slots, block_devices)
        arrived.append(swap(packed, devices))
    answers = []
    for m in range(micros):
        incoming = arrived[m].reshape(-1, width // PIECES)
        returned = run_expert(incoming, keep_limit, w_gate, w_up, w_down, slots, 2 * block_devices)
        answers.append(swap(returned, devices))
    out = None
    for m in range(micros):
        answered = answers[m].reshape(-1, width // PIECES)
        out = mix_answers(answered, expert_ids, gate_probs, m, slots, block_devices, out)
    return out


def solution(mesh):
    placed = (
        P(None, AXES, None),
        P(None, AXES, None),
        P(None, AXES, None),
        P(AXES),
        P(AXES, None),
        P(AXES, None, None),
        P(AXES, None, None),
        P(AXES, None, None),
    )
    return jax.shard_map(
        body,
        mesh=mesh,
        in_specs=placed,
        out_specs=P(None, AXES, None),
        check_vma=False,
    )
```

time: 518 us -> 305 us (0.59)
  the two profiles are of different devices: /device:TPU:90 before, /device:TPU:1 now
where the time goes in v1:
time: 305 us; the launch traced here: 304 us
  waiting for transfers between devices  178 us (58%)
  Pallas kernels  94 us (31%)
  starting transfers between devices  28.7 us (9%)
    all_to_all x4, waiting for transfers between devices, swap(): return lax.all_to_all(parts, AXES, split_axis=0, concat_axis=0, tiled=True)  178 us
    pallas_call x2, Pallas kernels, run_expert(): pl.pallas_call(kernel, grid=(steps,), in_specs=[pl.BlockSpec(memory_space...  56.8 us
    all_to_all x4, starting transfers between devices, swap(): return lax.all_to_all(parts, AXES, split_axis=0, concat_axis=0, tiled=True)  28.7 us
    pallas_call x2, Pallas kernels, mix_answers(): pl.pallas_call(kernel, grid=(steps,), in_specs=in_specs, out_specs=pl.Blo...  19.3 us
    pallas_call x2, Pallas kernels, pack_tokens(): pl.pallas_call(kernel, grid=(experts // block_devices,), in_specs=[pl.Blo...  17.9 us
  transfers between devices with their start and end apart: 4, of which 4 were waited for; matrix products, arithmetic and copies ran while one was open for 0% of the time, Pallas kernels for 25%

profile of v1, /device:TPU:1, one launch (start us, length us, event | category | flops | bytes accessed | tf_op | source)
XLA Modules:
  0.0 304.5 jit_solution(10896500410682988812)
XLA Ops:
  0.0 1.5 copy.14.ids_ref
  1.5 8.9 %pack_tokens.3 = bf16[5120,512]{1,0:T(8,128)(2,1)} custom-call(s32[2,128,8]{2,1,0:T(8,128)} %copy.14.ids_ref, bf16[2,128,2048]{2,1,0:T(8,128)(2,1)} %tok_ref.3), custom_call_target="tpu_custom_call" | custom-call | tf_op jit(solution)/shard_map/pack_tokens/pallas_call | solution.py:66
  10.4 11.9 %all-to-all-start.2 = ((bf16[128,40,512]{2,1,0:T(8,128)(2,1)}), bf16[128,40,512]{2,1,0:T(8,128)(2,1)}, u32[]{:S(2)}, u32[]{:S(2)}) async-start(bf16[128,40,512]{2,1,0:T(8,128)(2,1)} %bitcast.10), calls=%async_computation.2 | async-start | bytes 10485760 | tf_op jit(solution)/shard_map/all_to_all | solution.py:239
  22.3 9.0 %pack_tokens.2 = bf16[5120,512]{1,0:T(8,128)(2,1)} custom-call(s32[2,128,8]{2,1,0:T(8,128)} %copy.14.ids_ref, bf16[2,128,2048]{2,1,0:T(8,128)(2,1)} %tok_ref.3), custom_call_target="tpu_custom_call" | custom-call | tf_op jit(solution)/shard_map/pack_tokens/pallas_call | solution.py:66
  31.3 54.8 %all-to-all-done.2 = bf16[128,40,512]{2,1,0:T(8,128)(2,1)} async-done(((bf16[128,40,512]{2,1,0:T(8,128)(2,1)}), bf16[128,40,512]{2,1,0:T(8,128)(2,1)}, u32[]{:S(2)}, u32[]{:S(2)}) %all-to-all-start.2) | async-done | bytes 5242912 | tf_op jit(solution)/shard_map/all_to_all | solution.py:239
  86.1 0.0 copy-start.1
  86.1 5.7 %all-to-all-start = ((bf16[128,40,512]{2,1,0:T(8,128)(2,1)}), bf16[128,40,512]{2,1,0:T(8,128)(2,1)}, u32[]{:S(2)}, u32[]{:S(2)}) async-start(bf16[128,40,512]{2,1,0:T(8,128)(2,1)} %bitcast.9), calls=%async_computation | async-start | bytes 10485760 | tf_op jit(solution)/shard_map/all_to_all | solution.py:239
  92.4 0.0 copy-done.1
  92.4 0.6 reduce_sum.11
  93.7 28.4 %run_expert.3 = bf16[5120,512]{1,0:T(8,128)(2,1)} custom-call(s32[1]{0:T(128)S(6)} %add.3.limit_ref, bf16[5120,512]{1,0:T(8,128)(2,1)} %bitcast.6.in_ref, bf16[1,2048,768]{2,1,0:T(8,128)(2,1)} %gate_ref.3, bf16[1,2048,768]{2,1,0:T(8,128)(2,1)} %up_ref.3, bf16[1,768,2048]{2,1,0:T(8,128)(2,1)} %down_ref.3), custom_call_target="tpu_custom_call" | custom-call | tf_op jit(solution)/shard_map/run_expert/pallas_call | solution.py:215
  122.1 33.6 %all-to-all-done = bf16[128,40,512]{2,1,0:T(8,128)(2,1)} async-done(((bf16[128,40,512]{2,1,0:T(8,128)(2,1)}), bf16[128,40,512]{2,1,0:T(8,128)(2,1)}, u32[]{:S(2)}, u32[]{:S(2)}) %all-to-all-start) | async-done | bytes 5242912 | tf_op jit(solution)/shard_map/all_to_all | solution.py:239
  155.7 5.5 %all-to-all-start.3 = ((bf16[128,40,512]{2,1,0:T(8,128)(2,1)}), bf16[128,40,512]{2,1,0:T(8,128)(2,1)}, u32[]{:S(2)}, u32[]{:S(2)}) async-start(bf16[128,40,512]{2,1,0:T(8,128)(2,1)} %bitcast.12), calls=%async_computation.3 | async-start | bytes 10485760 | tf_op jit(solution)/shard_map/all_to_all | solution.py:239
  161.3 28.4 %run_expert.2 = bf16[5120,512]{1,0:T(8,128)(2,1)} custom-call(s32[1]{0:T(128)S(6)} %add.3.limit_ref, bf16[5120,512]{1,0:T(8,128)(2,1)} %bitcast.2.in_ref, bf16[1,2048,768]{2,1,0:T(8,128)(2,1)} %gate_ref.3, bf16[1,2048,768]{2,1,0:T(8,128)(2,1)} %up_ref.3, bf16[1,768,2048]{2,1,0:T(8,128)(2,1)} %down_ref.3), custom_call_target="tpu_custom_call" | custom-call | tf_op jit(solution)/shard_map/run_expert/pallas_call | solution.py:215
  189.7 35.5 %all-to-all-done.3 = bf16[128,40,512]{2,1,0:T(8,128)(2,1)} async-done(((bf16[128,40,512]{2,1,0:T(8,128)(2,1)}), bf16[128,40,512]{2,1,0:T(8,128)(2,1)}, u32[]{:S(2)}, u32[]{:S(2)}) %all-to-all-start.3) | async-done | bytes 5242912 | tf_op jit(solution)/shard_map/all_to_all | solution.py:239
  225.2 0.0 copy-start
  225.2 5.7 %all-to-all-start.1 = ((bf16[128,40,512]{2,1,0:T(8,128)(2,1)}), bf16[128,40,512]{2,1,0:T(8,128)(2,1)}, u32[]{:S(2)}, u32[]{:S(2)}) async-start(bf16[128,40,512]{2,1,0:T(8,128)(2,1)} %bitcast.11), calls=%async_computation.1 | async-start | bytes 10485760 | tf_op jit(solution)/shard_map/all_to_all | solution.py:239
  230.9 0.0 copy-done
  230.9 0.8 copy.15.probs_ref
  231.7 9.6 %mix_answers.2.rest_0_ = bf16[2,128,2048]{2,1,0:T(8,128)(2,1)} custom-call(s32[2,128,8]{2,1,0:T(8,128)} %copy.14.ids_ref, f32[2,128,8]{2,1,0:T(8,128)} %copy.15.probs_ref, bf16[5120,512]{1,0:T(8,128)(2,1)} %bitcast.8.rows_ref), custom_call_target="tpu_custom_call" | custom-call | tf_op jit(solution)/shard_map/mix_answers/pallas_call | solution.py:140
  241.3 53.5 %all-to-all-done.1 = bf16[128,40,512]{2,1,0:T(8,128)(2,1)} async-done(((bf16[128,40,512]{2,1,0:T(8,128)(2,1)}), bf16[128,40,512]{2,1,0:T(8,128)(2,1)}, u32[]{:S(2)}, u32[]{:S(2)}) %all-to-all-start.1) | async-done | bytes 5242912 | tf_op jit(solution)/shard_map/all_to_all | solution.py:239
  294.9 9.6 %mix_answers.3 = bf16[2,128,2048]{2,1,0:T(8,128)(2,1)} custom-call(s32[2,128,8]{2,1,0:T(8,128)} %copy.14.ids_ref, f32[2,128,8]{2,1,0:T(8,128)} %copy.15.probs_ref, bf16[5120,512]{1,0:T(8,128)(2,1)} %bitcast.4.rows_ref, bf16[2,128,2048]{2,1,0:T(8,128)(2,1)} %mix_answers.2.rest_0_), custom_call_target="tpu_custom_call", output_to_operand_aliasing={{}: (3, {})} | custom-call | tf_op jit(solution)/shard_map/mix_answers/pallas_call | solution.py:140
Async XLA Ops:
  10.4 75.7 %all-to-all-start.2 = ((bf16[128,40,512]{2,1,0:T(8,128)(2,1)}), bf16[128,40,512]{2,1,0:T(8,128)(2,1)}, u32[]{:S(2)}, u32[]{:S(2)}) async-start(bf16[128,40,512]{2,1,0:T(8,128)(2,1)} %bitcast.10), calls=%async_computation.2 | async-start | bytes 10485760 | tf_op jit(solution)/shard_map/all_to_all | solution.py:239
  86.1 6.3 %copy-start.1 = (s32[1,3]{1,0:T(1,128)S(1)}, s32[1,3]{1,0:T(1,128)}, u32[]{:S(2)}) copy-start(s32[1,3]{1,0:T(1,128)} %param.12) | copy-start | bytes 40
  86.1 69.6 %all-to-all-start = ((bf16[128,40,512]{2,1,0:T(8,128)(2,1)}), bf16[128,40,512]{2,1,0:T(8,128)(2,1)}, u32[]{:S(2)}, u32[]{:S(2)}) async-start(bf16[128,40,512]{2,1,0:T(8,128)(2,1)} %bitcast.9), calls=%async_computation | async-start | bytes 10485760 | tf_op jit(solution)/shard_map/all_to_all | solution.py:239
  155.7 69.5 %all-to-all-start.3 = ((bf16[128,40,512]{2,1,0:T(8,128)(2,1)}), bf16[128,40,512]{2,1,0:T(8,128)(2,1)}, u32[]{:S(2)}, u32[]{:S(2)}) async-start(bf16[128,40,512]{2,1,0:T(8,128)(2,1)} %bitcast.12), calls=%async_computation.3 | async-start | bytes 10485760 | tf_op jit(solution)/shard_map/all_to_all | solution.py:239
  225.2 5.7 %copy-start = (f32[2,128,8]{1,2,0:T(8,128)S(1)}, f32[2,128,8]{1,2,0:T(8,128)}, u32[]{:S(2)}) copy-start(f32[2,128,8]{1,2,0:T(8,128)} %param.10) | copy-start | bytes 24580
  225.2 69.6 %all-to-all-start.1 = ((bf16[128,40,512]{2,1,0:T(8,128)(2,1)}), bf16[128,40,512]{2,1,0:T(8,128)(2,1)}, u32[]{:S(2)}, u32[]{:S(2)}) async-start(bf16[128,40,512]{2,1,0:T(8,128)(2,1)} %bitcast.11), calls=%async_computation.1 | async-start | bytes 10485760 | tf_op jit(solution)/shard_map/all_to_all | solution.py:239

commit v2 on v1

v2 whole, which is shorter than its diff:
```python
import jax
import jax.numpy as jnp
from jax import lax
from jax.experimental import pallas as pl
from jax.experimental.pallas import tpu as pltpu
from jax.sharding import PartitionSpec as P

AXES = ("expert", "group")
PIECES = 4
TILE = 8
MARK = 8.0


def iota(shape, dim):
    return lax.broadcasted_iota(jnp.int32, shape, dim)


def bit(condition):
    return jnp.where(condition, 1.0, 0.0)


def narrow(x):
    return x.astype(jnp.bfloat16)


def mm(a, b):
    return jnp.dot(a, b, preferred_element_type=jnp.float32)


def chosen_rank(ids, experts):
    top, tok = ids.shape
    expert = iota((experts, tok), 0)
    chosen = jnp.zeros((experts, tok), jnp.float32)
    for k in range(top):
        chosen = jnp.where(ids[k : k + 1, :] == expert, 1.0, chosen)
    before = mm(narrow(chosen), narrow(bit(iota((tok, tok), 0) < iota((tok, tok), 1))))
    return chosen * (before + 1.0)


def pack_tokens(tokens, ids, micro, block):
    _, tok, width = tokens.shape
    top = ids.shape[1]
    experts = lax.axis_size(AXES)
    part = width // PIECES
    rows = block * TILE

    def kernel(ids_ref, tok_ref, out_ref, rank_ref, piece_ref):
        step = pl.program_id(0)

        @pl.when(step == 0)
        def _():
            rank_ref[...] = narrow(chosen_rank(ids_ref[0], experts))
            for q in range(PIECES):
                piece_ref[q * tok : (q + 1) * tok, :] = tok_ref[0, :, q * part : (q + 1) * part]

        row = iota((rows, experts), 0)
        col = iota((rows, experts), 1)
        spread = narrow(bit((row >> 3) + step * block == col))
        rank = mm(spread, rank_ref[...])
        inside = row & 7
        hit = bit(rank == (inside + 1).astype(jnp.float32))
        select = narrow(hit)
        first = col == 0
        mark = jnp.where((jnp.sum(hit, axis=1, keepdims=True) < 0.5) & first, MARK, 0.0)
        for q in range(PIECES):
            moved = mm(select, piece_ref[q * tok : (q + 1) * tok, :])
            if q == 0:
                moved = jnp.concatenate([moved[:, :experts] + mark, moved[:, experts:]], axis=1)
            out_ref[:, q] = narrow(moved.reshape(block, TILE, part))
        hit = bit(rank == ((inside >> 2) + (TILE + 1)).astype(jnp.float32))
        piece = inside & 3
        select = jnp.concatenate([narrow(jnp.where(piece == q, hit, 0.0)) for q in range(PIECES)], axis=1)
        moved = mm(select, piece_ref[...])
        mark = jnp.where((jnp.sum(hit, axis=1, keepdims=True) < 0.5) & first & (piece == 0), MARK, 0.0)
        moved = jnp.concatenate([moved[:, :experts] + mark, moved[:, experts:]], axis=1)
        out_ref[:, PIECES] = narrow(moved.reshape(block, TILE, part))

    shape = (PIECES + 1, TILE, part)
    return pl.pallas_call(
        kernel,
        grid=(experts // block,),
        in_specs=[
            pl.BlockSpec((1, top, tok), lambda i: (micro, 0, 0)),
            pl.BlockSpec((1, tok, width), lambda i: (micro, 0, 0)),
        ],
        out_specs=pl.BlockSpec((block, *shape), lambda i: (i, 0, 0, 0)),
        out_shape=jax.ShapeDtypeStruct((experts, *shape), jnp.bfloat16),
        scratch_shapes=[
            pltpu.VMEM((experts, tok), jnp.bfloat16),
            pltpu.VMEM((PIECES * tok, part), jnp.bfloat16),
        ],
        name="pack_tokens",
    )(ids, tokens)


def mix_answers(answered, ids, probs, micro, block, earlier_out):
    micros, top, tok = ids.shape
    experts = lax.axis_size(AXES)
    part = answered.shape[3]
    width = part * PIECES
    rows = block * TILE
    steps = experts // block

    def kernel(ids_ref, probs_ref, rows_ref, *rest):
        out_ref, rank_ref, gate_ref, sum_ref = rest[-4:]
        step = pl.program_id(0)

        @pl.when(step == 0)
        def _():
            ids_here = ids_ref[0]
            probs_here = probs_ref[0]
            norm = probs_here / jnp.sum(probs_here, axis=0, keepdims=True)
            expert = iota((experts, tok), 0)
            gate = jnp.zeros((experts, tok), jnp.float32)
            for k in range(top):
                gate = jnp.where(ids_here[k : k + 1, :] == expert, norm[k : k + 1, :], gate)
            gate_ref[...] = narrow(gate.T)
            rank_ref[...] = narrow(chosen_rank(ids_here, experts).T)
            sum_ref[...] = jnp.zeros_like(sum_ref)

        col = iota((experts, rows), 1)
        spread = narrow(bit((col >> 3) + step * block == iota((experts, rows), 0)))
        rank = mm(rank_ref[...], spread)
        gate = mm(gate_ref[...], spread)
        inside = iota((tok, rows), 1) & 7
        weight = narrow(jnp.where(rank == (inside + 1).astype(jnp.float32), gate, 0.0))
        rest_weight = jnp.where(rank == ((inside >> 2) + (TILE + 1)).astype(jnp.float32), gate, 0.0)
        last = rows_ref[:, PIECES].reshape(rows, part)
        for q in range(PIECES):
            mine = narrow(jnp.where((inside & 3) == q, rest_weight, 0.0))
            both = jnp.concatenate([weight, mine], axis=1)
            values = jnp.concatenate([rows_ref[:, q].reshape(rows, part), last], axis=0)
            sum_ref[:, q * part : (q + 1) * part] += mm(both, values)

        @pl.when(step == steps - 1)
        def _():
            out_ref[0] = narrow(sum_ref[...])

    in_specs = [
        pl.BlockSpec((1, top, tok), lambda i: (micro, 0, 0)),
        pl.BlockSpec((1, top, tok), lambda i: (micro, 0, 0)),
        pl.BlockSpec((block, PIECES + 1, TILE, part), lambda i: (i, 0, 0, 0)),
    ]
    operands = [ids, probs, answered]
    aliases = {}
    if earlier_out is not None:
        in_specs.append(pl.BlockSpec(memory_space=pl.ANY))
        operands.append(earlier_out)
        aliases = {3: 0}
    return pl.pallas_call(
        kernel,
        grid=(steps,),
        in_specs=in_specs,
        out_specs=pl.BlockSpec((1, tok, width), lambda i: (micro, 0, 0)),
        out_shape=jax.ShapeDtypeStruct((micros, tok, width), jnp.bfloat16),
        scratch_shapes=[
            pltpu.VMEM((tok, experts), jnp.bfloat16),
            pltpu.VMEM((tok, experts), jnp.bfloat16),
            pltpu.VMEM((tok, width), jnp.float32),
        ],
        input_output_aliases=aliases,
        name="mix_answers",
    )(*operands)


def place(row, slots, q):
    device = jnp.floor((row.astype(jnp.float32) + 0.5) * (1.0 / slots)).astype(jnp.int32)
    slot = row - device * slots
    inside = jnp.where(slot < TILE, q * TILE + slot, slot * PIECES + q)
    return device * slots * PIECES + inside


def run_expert(arrived, keep_limit, gate_mat, up_mat, down_mat, slots, block_devices):
    packed_rows, part = arrived.shape
    width, hidden_dim = gate_mat.shape[1:]
    turn = 16 * slots
    turns = block_devices * slots // turn
    rows = block_devices * slots
    steps = packed_rows // (rows * PIECES)

    def kernel(limit_ref, in_ref, gate_ref, up_ref, down_ref, out_ref, join_ref, split_ref, rows_ref, seen_ref):
        step = pl.program_id(0)

        @pl.when(step == 0)
        def _():
            seen_ref[...] = jnp.zeros_like(seen_ref)
            for q in range(PIECES):
                shape = (turn, turn * PIECES)
                join_ref[q] = narrow(bit(place(iota(shape, 0), slots, q) == iota(shape, 1)))
                shape = (turn * PIECES, turn)
                split_ref[q] = narrow(bit(place(iota(shape, 1), slots, q) == iota(shape, 0)))

        for j in range(turns):
            pieces = in_ref[j * turn * PIECES : (j + 1) * turn * PIECES, :]
            for q in range(PIECES):
                rows_ref[j * turn : (j + 1) * turn, q * part : (q + 1) * part] = jnp.dot(
                    join_ref[q], pieces, preferred_element_type=jnp.float32
                ).astype(jnp.bfloat16)
        rows_here = rows_ref[...]
        lanes = seen_ref.shape[1]
        live = jnp.where(
            jnp.broadcast_to(rows_here[:, :1].astype(jnp.float32), (rows, lanes)) < MARK - 1.0, 1.0, 0.0
        )
        above = lax.broadcasted_iota(jnp.int32, (rows, rows), 0) > lax.broadcasted_iota(jnp.int32, (rows, rows), 1)
        rank = seen_ref[...] + jnp.dot(
            jnp.where(above, 1.0, 0.0).astype(jnp.bfloat16),
            live.astype(jnp.bfloat16),
            preferred_element_type=jnp.float32,
        )
        seen_ref[...] += jnp.sum(live, axis=0, keepdims=True)
        limit = limit_ref[0].astype(jnp.float32)
        kept = (live > 0.5) & (rank < limit)
        kept = jnp.where(kept, 1.0, 0.0)[:, :1] > 0.5

        gate_val = jnp.dot(rows_here, gate_ref[0], preferred_element_type=jnp.float32)
        up_val = jnp.dot(rows_here, up_ref[0], preferred_element_type=jnp.float32)
        hidden = (gate_val * lax.logistic(gate_val) * up_val).astype(jnp.bfloat16)
        out_val = jnp.dot(hidden, down_ref[0], preferred_element_type=jnp.float32)
        out_val = jnp.where(kept, out_val, 0.0).astype(jnp.bfloat16)
        for j in range(turns):
            moved = jnp.zeros((turn * PIECES, part), jnp.float32)
            for q in range(PIECES):
                moved = moved + jnp.dot(
                    split_ref[q],
                    out_val[j * turn : (j + 1) * turn, q * part : (q + 1) * part],
                    preferred_element_type=jnp.float32,
                )
            out_ref[j * turn * PIECES : (j + 1) * turn * PIECES, :] = moved.astype(jnp.bfloat16)

    return pl.pallas_call(
        kernel,
        grid=(steps,),
        in_specs=[
            pl.BlockSpec(memory_space=pltpu.SMEM),
            pl.BlockSpec((rows * PIECES, part), lambda i: (i, 0)),
            pl.BlockSpec((1, width, hidden_dim), lambda i: (0, 0, 0)),
            pl.BlockSpec((1, width, hidden_dim), lambda i: (0, 0, 0)),
            pl.BlockSpec((1, hidden_dim, width), lambda i: (0, 0, 0)),
        ],
        out_specs=pl.BlockSpec((rows * PIECES, part), lambda i: (i, 0)),
        out_shape=jax.ShapeDtypeStruct((packed_rows, part), jnp.bfloat16),
        scratch_shapes=[
            pltpu.VMEM((PIECES, turn, turn * PIECES), jnp.bfloat16),
            pltpu.VMEM((PIECES, turn * PIECES, turn), jnp.bfloat16),
            pltpu.VMEM((rows, width), jnp.bfloat16),
            pltpu.VMEM((1, 128), jnp.float32),
        ],
        name="run_expert",
    )(keep_limit, arrived, gate_mat, up_mat, down_mat)


def swap(rows, devices):
    parts = rows.reshape(devices, -1, rows.shape[-1])
    return lax.all_to_all(parts, AXES, split_axis=0, concat_axis=0, tiled=True)


def body(tokens, expert_ids, gate_probs, capacity, flows, w_gate, w_up, w_down):
    devices = lax.axis_size(AXES)
    micros, tok, width = tokens.shape
    top = expert_ids.shape[2]
    ids = jnp.swapaxes(expert_ids, 1, 2)
    probs = jnp.swapaxes(gate_probs, 1, 2)
    slots = tok * top * 5 // (4 * devices)
    block_devices = 64
    keep_limit = capacity + jnp.sum(flows, 1)

    arrived = []
    for m in range(micros):
        packed = pack_tokens(tokens, ids, m, block_devices)
        arrived.append(swap(packed, devices))
    answers = []
    for m in range(micros):
        incoming = arrived[m].reshape(-1, width // PIECES)
        returned = run_expert(incoming, keep_limit, w_gate, w_up, w_down, slots, block_devices // 2)
        answers.append(swap(returned, devices))
    out = None
    for m in range(micros):
        answered = answers[m].reshape(devices, PIECES + 1, TILE, width // PIECES)
        out = mix_answers(answered, ids, probs, m, block_devices, out)
    return out


def solution(mesh):
    placed = (
        P(None, AXES, None),
        P(None, AXES, None),
        P(None, AXES, None),
        P(AXES),
        P(AXES, None),
        P(AXES, None, None),
        P(AXES, None, None),
        P(AXES, None, None),
    )
    return jax.shard_map(
        body,
        mesh=mesh,
        in_specs=placed,
        out_specs=P(None, AXES, None),
        check_vma=False,
    )
```

time: 305 us -> 295 us (0.967)
  Pallas kernels: 94 us -> 76.5 us
  waiting for transfers between devices: 178 us -> 187 us
    pallas_call x2, Pallas kernels: 19.3 us -> 9.45 us  [mix_answers(): pl.pallas_call(kernel, grid=(steps,), in_specs=in_specs, out_specs=pl.Blo...]
    all_to_all x4, waiting for transfers between devices: 178 us -> 187 us  [swap(): return lax.all_to_all(parts, AXES, split_axis=0, concat_axis=0, tiled=True)]
    pallas_call x2, Pallas kernels: 17.9 us -> 9.95 us  [pack_tokens(): pl.pallas_call(kernel, grid=(experts // block,), in_specs=[pl.BlockSpec((...]
  transfers between devices with their start and end apart: 4 -> 4, of which waited for: 4 -> 4; matrix products, arithmetic and copies ran while one was open for 0% -> 0% of each run, Pallas kernels for 25% -> 23%
where the time goes in v2:
time: 295 us; the launch traced here: 294 us
  waiting for transfers between devices  187 us (63%)
  Pallas kernels  76.5 us (26%)
  starting transfers between devices  28.6 us (10%)
    all_to_all x4, waiting for transfers between devices, swap(): return lax.all_to_all(parts, AXES, split_axis=0, concat_axis=0, tiled=True)  187 us
    pallas_call x2, Pallas kernels, run_expert(): pl.pallas_call(kernel, grid=(steps,), in_specs=[pl.BlockSpec(memory_space...  57.1 us
    all_to_all x4, starting transfers between devices, swap(): return lax.all_to_all(parts, AXES, split_axis=0, concat_axis=0, tiled=True)  28.6 us
    pallas_call x2, Pallas kernels, pack_tokens(): pl.pallas_call(kernel, grid=(experts // block,), in_specs=[pl.BlockSpec((...  9.95 us
    pallas_call x2, Pallas kernels, mix_answers(): pl.pallas_call(kernel, grid=(steps,), in_specs=in_specs, out_specs=pl.Blo...  9.45 us
  transfers between devices with their start and end apart: 4, of which 4 were waited for; matrix products, arithmetic and copies ran while one was open for 0% of the time, Pallas kernels for 23%

profile of v2, /device:TPU:1, one launch (start us, length us, event | category | flops | bytes accessed | tf_op | source)
XLA Modules:
  0.0 294.1 jit_solution(4414372948714390909)
XLA Ops:
  0.0 5.0 %pack_tokens.3 = bf16[128,5,8,512]{3,2,1,0:T(8,128)(2,1)} custom-call(s32[2,8,128]{2,1,0:T(8,128)} %bitcast.15, bf16[2,128,2048]{2,1,0:T(8,128)(2,1)} %tok_ref.3), custom_call_target="tpu_custom_call" | custom-call | tf_op jit(solution)/shard_map/pack_tokens/pallas_call | solution.py:79
  5.0 11.9 %all-to-all-start.2 = ((bf16[128,40,512]{2,1,0:T(8,128)(2,1)}), bf16[128,40,512]{2,1,0:T(8,128)(2,1)}, u32[]{:S(2)}, u32[]{:S(2)}) async-start(bf16[128,40,512]{2,1,0:T(8,128)(2,1)} %bitcast.12), calls=%async_computation.2 | async-start | bytes 10485760 | tf_op jit(solution)/shard_map/all_to_all | solution.py:254
  16.9 5.0 %pack_tokens.2 = bf16[128,5,8,512]{3,2,1,0:T(8,128)(2,1)} custom-call(s32[2,8,128]{2,1,0:T(8,128)} %bitcast.16, bf16[2,128,2048]{2,1,0:T(8,128)(2,1)} %tok_ref.3), custom_call_target="tpu_custom_call" | custom-call | tf_op jit(solution)/shard_map/pack_tokens/pallas_call | solution.py:79
  21.8 58.9 %all-to-all-done.2 = bf16[128,40,512]{2,1,0:T(8,128)(2,1)} async-done(((bf16[128,40,512]{2,1,0:T(8,128)(2,1)}), bf16[128,40,512]{2,1,0:T(8,128)(2,1)}, u32[]{:S(2)}, u32[]{:S(2)}) %all-to-all-start.2) | async-done | bytes 5242912 | tf_op jit(solution)/shard_map/all_to_all | solution.py:254
  80.7 0.0 copy-start
  80.7 5.7 %all-to-all-start = ((bf16[128,40,512]{2,1,0:T(8,128)(2,1)}), bf16[128,40,512]{2,1,0:T(8,128)(2,1)}, u32[]{:S(2)}, u32[]{:S(2)}) async-start(bf16[128,40,512]{2,1,0:T(8,128)(2,1)} %bitcast.11), calls=%async_computation | async-start | bytes 10485760 | tf_op jit(solution)/shard_map/all_to_all | solution.py:254
  87.0 0.0 copy-done
  87.0 0.6 reduce_sum.11
  88.3 28.5 %run_expert.3 = bf16[5120,512]{1,0:T(8,128)(2,1)} custom-call(s32[1]{0:T(128)S(6)} %add.3.limit_ref, bf16[5120,512]{1,0:T(8,128)(2,1)} %bitcast.8.in_ref, bf16[1,2048,768]{2,1,0:T(8,128)(2,1)} %gate_ref.3, bf16[1,2048,768]{2,1,0:T(8,128)(2,1)} %up_ref.3, bf16[1,768,2048]{2,1,0:T(8,128)(2,1)} %down_ref.3), custom_call_target="tpu_custom_call" | custom-call | tf_op jit(solution)/shard_map/run_expert/pallas_call | solution.py:230
  116.8 33.5 %all-to-all-done = bf16[128,40,512]{2,1,0:T(8,128)(2,1)} async-done(((bf16[128,40,512]{2,1,0:T(8,128)(2,1)}), bf16[128,40,512]{2,1,0:T(8,128)(2,1)}, u32[]{:S(2)}, u32[]{:S(2)}) %all-to-all-start) | async-done | bytes 5242912 | tf_op jit(solution)/shard_map/all_to_all | solution.py:254
  150.3 5.5 %all-to-all-start.3 = ((bf16[128,40,512]{2,1,0:T(8,128)(2,1)}), bf16[128,40,512]{2,1,0:T(8,128)(2,1)}, u32[]{:S(2)}, u32[]{:S(2)}) async-start(bf16[128,40,512]{2,1,0:T(8,128)(2,1)} %bitcast.13), calls=%async_computation.3 | async-start | bytes 10485760 | tf_op jit(solution)/shard_map/all_to_all | solution.py:254
  155.9 28.5 %run_expert.2 = bf16[5120,512]{1,0:T(8,128)(2,1)} custom-call(s32[1]{0:T(128)S(6)} %add.3.limit_ref, bf16[5120,512]{1,0:T(8,128)(2,1)} %bitcast.4.in_ref, bf16[1,2048,768]{2,1,0:T(8,128)(2,1)} %gate_ref.3, bf16[1,2048,768]{2,1,0:T(8,128)(2,1)} %up_ref.3, bf16[1,768,2048]{2,1,0:T(8,128)(2,1)} %down_ref.3), custom_call_target="tpu_custom_call" | custom-call | tf_op jit(solution)/shard_map/run_expert/pallas_call | solution.py:230
  184.4 35.4 %all-to-all-done.3 = bf16[128,40,512]{2,1,0:T(8,128)(2,1)} async-done(((bf16[128,40,512]{2,1,0:T(8,128)(2,1)}), bf16[128,40,512]{2,1,0:T(8,128)(2,1)}, u32[]{:S(2)}, u32[]{:S(2)}) %all-to-all-start.3) | async-done | bytes 5242912 | tf_op jit(solution)/shard_map/all_to_all | solution.py:254
  219.8 5.5 %all-to-all-start.1 = ((bf16[128,40,512]{2,1,0:T(8,128)(2,1)}), bf16[128,40,512]{2,1,0:T(8,128)(2,1)}, u32[]{:S(2)}, u32[]{:S(2)}) async-start(bf16[128,40,512]{2,1,0:T(8,128)(2,1)} %bitcast.14), calls=%async_computation.1 | async-start | bytes 10485760 | tf_op jit(solution)/shard_map/all_to_all | solution.py:254
  225.4 4.7 %mix_answers.2.rest_0_ = bf16[2,128,2048]{2,1,0:T(8,128)(2,1)} custom-call(s32[2,8,128]{2,1,0:T(8,128)} %bitcast.17, f32[2,8,128]{2,1,0:T(8,128)} %bitcast.19, bf16[128,5,8,512]{3,2,1,0:T(8,128)(2,1)} %bitcast.10.rows_ref), custom_call_target="tpu_custom_call" | custom-call | tf_op jit(solution)/shard_map/mix_answers/pallas_call | solution.py:150
  230.1 59.2 %all-to-all-done.1 = bf16[128,40,512]{2,1,0:T(8,128)(2,1)} async-done(((bf16[128,40,512]{2,1,0:T(8,128)(2,1)}), bf16[128,40,512]{2,1,0:T(8,128)(2,1)}, u32[]{:S(2)}, u32[]{:S(2)}) %all-to-all-start.1) | async-done | bytes 5242912 | tf_op jit(solution)/shard_map/all_to_all | solution.py:254
  289.3 4.7 %mix_answers.3 = bf16[2,128,2048]{2,1,0:T(8,128)(2,1)} custom-call(s32[2,8,128]{2,1,0:T(8,128)} %bitcast.18, f32[2,8,128]{2,1,0:T(8,128)} %bitcast.20, bf16[128,5,8,512]{3,2,1,0:T(8,128)(2,1)} %bitcast.6.rows_ref, bf16[2,128,2048]{2,1,0:T(8,128)(2,1)} %mix_answers.2.rest_0_), custom_call_target="tpu_custom_call", output_to_operand_aliasing={{}: (3, {})} | custom-call | tf_op jit(solution)/shard_map/mix_answers/pallas_call | solution.py:150
Async XLA Ops:
  5.0 75.7 %all-to-all-start.2 = ((bf16[128,40,512]{2,1,0:T(8,128)(2,1)}), bf16[128,40,512]{2,1,0:T(8,128)(2,1)}, u32[]{:S(2)}, u32[]{:S(2)}) async-start(bf16[128,40,512]{2,1,0:T(8,128)(2,1)} %bitcast.12), calls=%async_computation.2 | async-start | bytes 10485760 | tf_op jit(solution)/shard_map/all_to_all | solution.py:254
  80.7 6.3 %copy-start = (s32[1,3]{1,0:T(1,128)S(1)}, s32[1,3]{1,0:T(1,128)}, u32[]{:S(2)}) copy-start(s32[1,3]{1,0:T(1,128)} %param.12) | copy-start | bytes 40
  80.7 69.6 %all-to-all-start = ((bf16[128,40,512]{2,1,0:T(8,128)(2,1)}), bf16[128,40,512]{2,1,0:T(8,128)(2,1)}, u32[]{:S(2)}, u32[]{:S(2)}) async-start(bf16[128,40,512]{2,1,0:T(8,128)(2,1)} %bitcast.11), calls=%async_computation | async-start | bytes 10485760 | tf_op jit(solution)/shard_map/all_to_all | solution.py:254
  150.3 69.5 %all-to-all-start.3 = ((bf16[128,40,512]{2,1,0:T(8,128)(2,1)}), bf16[128,40,512]{2,1,0:T(8,128)(2,1)}, u32[]{:S(2)}, u32[]{:S(2)}) async-start(bf16[128,40,512]{2,1,0:T(8,128)(2,1)} %bitcast.13), calls=%async_computation.3 | async-start | bytes 10485760 | tf_op jit(solution)/shard_map/all_to_all | solution.py:254
  219.8 69.5 %all-to-all-start.1 = ((bf16[128,40,512]{2,1,0:T(8,128)(2,1)}), bf16[128,40,512]{2,1,0:T(8,128)(2,1)}, u32[]{:S(2)}, u32[]{:S(2)}) async-start(bf16[128,40,512]{2,1,0:T(8,128)(2,1)} %bitcast.14), calls=%async_computation.1 | async-start | bytes 10485760 | tf_op jit(solution)/shard_map/all_to_all | solution.py:254

commit v3 on v2

--- a/solution.py
+++ b/solution.py
@@ -37,110 +37,112 @@
     return chosen * (before + 1.0)
 
 
-def pack_tokens(tokens, ids, micro, block):
+def pack_tokens(tokens, ids, micro):
     _, tok, width = tokens.shape
     top = ids.shape[1]
     experts = lax.axis_size(AXES)
     part = width // PIECES
-    rows = block * TILE
-
-    def kernel(ids_ref, tok_ref, out_ref, rank_ref, piece_ref):
-        step = pl.program_id(0)
-
-        @pl.when(step == 0)
-        def _():
-            rank_ref[...] = narrow(chosen_rank(ids_ref[0], experts))
-            for q in range(PIECES):
-                piece_ref[q * tok : (q + 1) * tok, :] = tok_ref[0, :, q * part : (q + 1) * part]
-
+    rows = experts * TILE
+
+    def kernel(ids_ref, tok_ref, out_ref, sent_ref, my_ids_ref, my_tok_ref, sems):
+        def leave(q):
+            return pltpu.make_async_copy(sent_ref.at[q], out_ref.at[:, q], sems.at[q])
+
+        get_ids = pltpu.make_async_copy(ids_ref.at[micro], my_ids_ref, sems.at[PIECES + 1])
+        get_ids.start()
+
+        get_tokens = pltpu.make_async_copy(tok_ref.at[micro], my_tok_ref, sems.at[PIECES + 2])
+        get_tokens.start()
+        get_ids.wait()
+        order = narrow(chosen_rank(my_ids_ref[...], experts))
         row = iota((rows, experts), 0)
         col = iota((rows, experts), 1)
-        spread = narrow(bit((row >> 3) + step * block == col))
-        rank = mm(spread, rank_ref[...])
+        rank = mm(narrow(bit((row >> 3) == col)), order)
         inside = row & 7
         hit = bit(rank == (inside + 1).astype(jnp.float32))
         select = narrow(hit)
         first = col == 0
         mark = jnp.where((jnp.sum(hit, axis=1, keepdims=True) < 0.5) & first, MARK, 0.0)
+        get_tokens.wait()
         for q in range(PIECES):
-            moved = mm(select, piece_ref[q * tok : (q + 1) * tok, :])
+            moved = mm(select, my_tok_ref[:, q * part : (q + 1) * part])
             if q == 0:
                 moved = jnp.concatenate([moved[:, :experts] + mark, moved[:, experts:]], axis=1)
-            out_ref[:, q] = narrow(moved.reshape(block, TILE, part))
+            sent_ref[q] = narrow(moved.reshape(experts, TILE, part))
+            leave(q).start()
         hit = bit(rank == ((inside >> 2) + (TILE + 1)).astype(jnp.float32))
         piece = inside & 3
         select = jnp.concatenate([narrow(jnp.where(piece == q, hit, 0.0)) for q in range(PIECES)], axis=1)
-        moved = mm(select, piece_ref[...])
+        stacked = jnp.concatenate([my_tok_ref[:, q * part : (q + 1) * part] for q in range(PIECES)], axis=0)
+        moved = mm(select, stacked)
         mark = jnp.where((jnp.sum(hit, axis=1, keepdims=True) < 0.5) & first & (piece == 0), MARK, 0.0)
         moved = jnp.concatenate([moved[:, :experts] + mark, moved[:, experts:]], axis=1)
-        out_ref[:, PIECES] = narrow(moved.reshape(block, TILE, part))
-
-    shape = (PIECES + 1, TILE, part)
+        sent_ref[PIECES] = narrow(moved.reshape(experts, TILE, part))
+        leave(PIECES).start()
+        for q in range(PIECES + 1):
+            leave(q).wait()
+
     return pl.pallas_call(
         kernel,
-        grid=(experts // block,),
-        in_specs=[
-            pl.BlockSpec((1, top, tok), lambda i: (micro, 0, 0)),
-            pl.BlockSpec((1, tok, width), lambda i: (micro, 0, 0)),
-        ],
-        out_specs=pl.BlockSpec((block, *shape), lambda i: (i, 0, 0, 0)),
-        out_shape=jax.ShapeDtypeStruct((experts, *shape), jnp.bfloat16),
+        grid=(1,),
+        in_specs=[pl.BlockSpec(memory_space=pl.ANY)] * 2,
+        out_specs=pl.BlockSpec(memory_space=pl.ANY),
+        out_shape=jax.ShapeDtypeStruct((experts, PIECES + 1, TILE, part), jnp.bfloat16),
         scratch_shapes=[
-            pltpu.VMEM((experts, tok), jnp.bfloat16),
-            pltpu.VMEM((PIECES * tok, part), jnp.bfloat16),
+            pltpu.VMEM((PIECES + 1, experts, TILE, part), jnp.bfloat16),
+            pltpu.VMEM((top, tok), ids.dtype),
+            pltpu.VMEM((tok, width), jnp.bfloat16),
+            pltpu.SemaphoreType.DMA((PIECES + 3,)),
         ],
         name="pack_tokens",
     )(ids, tokens)
 
 
-def mix_answers(answered, ids, probs, micro, block, earlier_out):
+def mix_answers(answered, ids, probs, micro, earlier_out):
     micros, top, tok = ids.shape
     experts = lax.axis_size(AXES)
     part = answered.shape[3]
     width = part * PIECES
-    rows = block * TILE
-    steps = experts // block
+    rows = experts * TILE
 
     def kernel(ids_ref, probs_ref, rows_ref, *rest):
-        out_ref, rank_ref, gate_ref, sum_ref = rest[-4:]
-        step = pl.program_id(0)
-
-        @pl.when(step == 0)
-        def _():
-            ids_here = ids_ref[0]
-            probs_here = probs_ref[0]
-            norm = probs_here / jnp.sum(probs_here, axis=0, keepdims=True)
-            expert = iota((experts, tok), 0)
-            gate = jnp.zeros((experts, tok), jnp.float32)
-            for k in range(top):
-                gate = jnp.where(ids_here[k : k + 1, :] == expert, norm[k : k + 1, :], gate)
-            gate_ref[...] = narrow(gate.T)
-            rank_ref[...] = narrow(chosen_rank(ids_here, experts).T)
-            sum_ref[...] = jnp.zeros_like(sum_ref)
-
-        col = iota((experts, rows), 1)
-        spread = narrow(bit((col >> 3) + step * block == iota((experts, rows), 0)))
-        rank = mm(rank_ref[...], spread)
-        gate = mm(gate_ref[...], spread)
+        out_ref, here_ref, my_ids_ref, my_probs_ref, sems = rest[-5:]
+
+        def fetch(q):
+            return pltpu.make_async_copy(rows_ref.at[:, q], here_ref.at[q], sems.at[q])
+
+        get_ids = pltpu.make_async_copy(ids_ref.at[micro], my_ids_ref, sems.at[PIECES + 1])
+        get_probs = pltpu.make_async_copy(probs_ref.at[micro], my_probs_ref, sems.at[PIECES + 2])
+        get_ids.start()
+        get_probs.start()
+        for q in (PIECES, *range(PIECES)):
+            fetch(q).start()
+        get_ids.wait()
+        get_probs.wait()
+        ids_here = my_ids_ref[...]
+        probs_here = my_probs_ref[...]
+        norm = probs_here / jnp.sum(probs_here, axis=0, keepdims=True)
+        expert = iota((experts, tok), 0)
+        gate = jnp.zeros((experts, tok), jnp.float32)
+        for k in range(top):
+            gate = jnp.where(ids_here[k : k + 1, :] == expert, norm[k : k + 1, :], gate)
+        spread = narrow(bit((iota((experts, rows), 1) >> 3) == iota((experts, rows), 0)))
+        rank = mm(narrow(chosen_rank(ids_here, experts).T), spread)
+        gate = mm(narrow(gate.T), spread)
         inside = iota((tok, rows), 1) & 7
         weight = narrow(jnp.where(rank == (inside + 1).astype(jnp.float32), gate, 0.0))
         rest_weight = jnp.where(rank == ((inside >> 2) + (TILE + 1)).astype(jnp.float32), gate, 0.0)
-        last = rows_ref[:, PIECES].reshape(rows, part)
+        rest_weight = jnp.concatenate(
+            [narrow(jnp.where((inside & 3) == q, rest_weight, 0.0)) for q in range(PIECES)], axis=0
+        )
+        fetch(PIECES).wait()
+        last = mm(rest_weight, here_ref[PIECES].reshape(rows, part))
         for q in range(PIECES):
-            mine = narrow(jnp.where((inside & 3) == q, rest_weight, 0.0))
-            both = jnp.concatenate([weight, mine], axis=1)
-            values = jnp.concatenate([rows_ref[:, q].reshape(rows, part), last], axis=0)
-            sum_ref[:, q * part : (q + 1) * part] += mm(both, values)
-
-        @pl.when(step == steps - 1)
-        def _():
-            out_ref[0] = narrow(sum_ref[...])
-
-    in_specs = [
-        pl.BlockSpec((1, top, tok), lambda i: (micro, 0, 0)),
-        pl.BlockSpec((1, top, tok), lambda i: (micro, 0, 0)),
-        pl.BlockSpec((block, PIECES + 1, TILE, part), lambda i: (i, 0, 0, 0)),
-    ]
+            fetch(q).wait()
+            main = mm(weight, here_ref[q].reshape(rows, part))
+            out_ref[0, :, q * part : (q + 1) * part] = narrow(main + last[q * tok : (q + 1) * tok])
+
+    in_specs = [pl.BlockSpec(memory_space=pl.ANY)] * 3
     operands = [ids, probs, answered]
     aliases = {}
     if earlier_out is not None:
@@ -149,14 +151,15 @@
         aliases = {3: 0}
     return pl.pallas_call(
         kernel,
-        grid=(steps,),
+        grid=(1,),
         in_specs=in_specs,
         out_specs=pl.BlockSpec((1, tok, width), lambda i: (micro, 0, 0)),
         out_shape=jax.ShapeDtypeStruct((micros, tok, width), jnp.bfloat16),
         scratch_shapes=[
-            pltpu.VMEM((tok, experts), jnp.bfloat16),
-            pltpu.VMEM((tok, experts), jnp.bfloat16),
-            pltpu.VMEM((tok, width), jnp.float32),
+            pltpu.VMEM((PIECES + 1, experts, TILE, part), jnp.bfloat16),
+            pltpu.VMEM((top, tok), ids.dtype),
+            pltpu.VMEM((top, tok), probs.dtype),
+            pltpu.SemaphoreType.DMA((PIECES + 3,)),
         ],
         input_output_aliases=aliases,
         name="mix_answers",
@@ -261,22 +264,22 @@
     ids = jnp.swapaxes(expert_ids, 1, 2)
     probs = jnp.swapaxes(gate_probs, 1, 2)
     slots = tok * top * 5 // (4 * devices)
-    block_devices = 64
+    block_devices = 32
     keep_limit = capacity + jnp.sum(flows, 1)
 
     arrived = []
     for m in range(micros):
-        packed = pack_tokens(tokens, ids, m, block_devices)
+        packed = pack_tokens(tokens, ids, m)
         arrived.append(swap(packed, devices))
     answers = []
     for m in range(micros):
         incoming = arrived[m].reshape(-1, width // PIECES)
-        returned = run_expert(incoming, keep_limit, w_gate, w_up, w_down, slots, block_devices // 2)
+        returned = run_expert(incoming, keep_limit, w_gate, w_up, w_down, slots, block_devices)
         answers.append(swap(returned, devices))
     out = None
     for m in range(micros):
         answered = answers[m].reshape(devices, PIECES + 1, TILE, width // PIECES)
-        out = mix_answers(answered, ids, probs, m, block_devices, out)
+        out = mix_answers(answered, ids, probs, m, out)
     return out
 
 

time: 295 us -> 293 us (level)
  Pallas kernels: 76.5 us -> 73.3 us
    pallas_call x4, Pallas kernels: 19.4 us -> 16.2 us  [the longest x2 8.28 us: pack_tokens(): pl.pallas_call(kernel, grid=(1,), in_specs=[pl.BlockSpec(memory_space=pl....]
  transfers between devices with their start and end apart: 4 -> 4, of which waited for: 4 -> 4; matrix products, arithmetic and copies ran while one was open for 0% -> 0% of each run, Pallas kernels for 23% -> 22%
where the time goes in v3:
time: 293 us
  waiting for transfers between devices  189 us (65%)
  Pallas kernels  73.3 us (25%)
  starting transfers between devices  28.6 us (10%)
    all_to_all x4, waiting for transfers between devices, swap(): return lax.all_to_all(parts, AXES, split_axis=0, concat_axis=0, tiled=True)  189 us
    pallas_call x2, Pallas kernels, run_expert(): pl.pallas_call(kernel, grid=(steps,), in_specs=[pl.BlockSpec(memory_space...  57.1 us
    all_to_all x4, starting transfers between devices, swap(): return lax.all_to_all(parts, AXES, split_axis=0, concat_axis=0, tiled=True)  28.6 us
    pallas_call x2, Pallas kernels, pack_tokens(): pl.pallas_call(kernel, grid=(1,), in_specs=[pl.BlockSpec(memory_space=pl....  8.28 us
    pallas_call x2, Pallas kernels, mix_answers(): pl.pallas_call(kernel, grid=(1,), in_specs=in_specs, out_specs=pl.BlockSp...  7.94 us
  transfers between devices with their start and end apart: 4, of which 4 were waited for; matrix products, arithmetic and copies ran while one was open for 0% of the time, Pallas kernels for 22%

profile of v3, /device:TPU:1, one launch (start us, length us, event | category | flops | bytes accessed | tf_op | source)
XLA Modules:
  0.0 292.7 jit_solution(13980746845770781265)
XLA Ops:
  0.0 4.2 %pack_tokens.3 = bf16[128,5,8,512]{3,2,1,0:T(8,128)(2,1)} custom-call(s32[2,8,128]{2,1,0:T(8,128)} %bitcast.15, bf16[2,128,2048]{2,1,0:T(8,128)(2,1)} %tok_ref.3), custom_call_target="tpu_custom_call" | custom-call | tf_op jit(solution)/shard_map/pack_tokens/pallas_call | solution.py:85
  4.2 11.9 %all-to-all-start.2 = ((bf16[128,40,512]{2,1,0:T(8,128)(2,1)}), bf16[128,40,512]{2,1,0:T(8,128)(2,1)}, u32[]{:S(2)}, u32[]{:S(2)}) async-start(bf16[128,40,512]{2,1,0:T(8,128)(2,1)} %bitcast.12), calls=%async_computation.2 | async-start | bytes 10485760 | tf_op jit(solution)/shard_map/all_to_all | solution.py:257
  16.1 4.1 %pack_tokens.2 = bf16[128,5,8,512]{3,2,1,0:T(8,128)(2,1)} custom-call(s32[2,8,128]{2,1,0:T(8,128)} %bitcast.16, bf16[2,128,2048]{2,1,0:T(8,128)(2,1)} %tok_ref.3), custom_call_target="tpu_custom_call" | custom-call | tf_op jit(solution)/shard_map/pack_tokens/pallas_call | solution.py:85
  20.2 59.7 %all-to-all-done.2 = bf16[128,40,512]{2,1,0:T(8,128)(2,1)} async-done(((bf16[128,40,512]{2,1,0:T(8,128)(2,1)}), bf16[128,40,512]{2,1,0:T(8,128)(2,1)}, u32[]{:S(2)}, u32[]{:S(2)}) %all-to-all-start.2) | async-done | bytes 5242912 | tf_op jit(solution)/shard_map/all_to_all | solution.py:257
  79.9 0.0 copy-start
  79.9 5.7 %all-to-all-start = ((bf16[128,40,512]{2,1,0:T(8,128)(2,1)}), bf16[128,40,512]{2,1,0:T(8,128)(2,1)}, u32[]{:S(2)}, u32[]{:S(2)}) async-start(bf16[128,40,512]{2,1,0:T(8,128)(2,1)} %bitcast.11), calls=%async_computation | async-start | bytes 10485760 | tf_op jit(solution)/shard_map/all_to_all | solution.py:257
  86.2 0.0 copy-done
  86.2 0.6 reduce_sum.11
  87.5 28.5 %run_expert.3 = bf16[5120,512]{1,0:T(8,128)(2,1)} custom-call(s32[1]{0:T(128)S(6)} %add.3.limit_ref, bf16[5120,512]{1,0:T(8,128)(2,1)} %bitcast.8.in_ref, bf16[1,2048,768]{2,1,0:T(8,128)(2,1)} %gate_ref.3, bf16[1,2048,768]{2,1,0:T(8,128)(2,1)} %up_ref.3, bf16[1,768,2048]{2,1,0:T(8,128)(2,1)} %down_ref.3), custom_call_target="tpu_custom_call" | custom-call | tf_op jit(solution)/shard_map/run_expert/pallas_call | solution.py:233
  116.0 33.5 %all-to-all-done = bf16[128,40,512]{2,1,0:T(8,128)(2,1)} async-done(((bf16[128,40,512]{2,1,0:T(8,128)(2,1)}), bf16[128,40,512]{2,1,0:T(8,128)(2,1)}, u32[]{:S(2)}, u32[]{:S(2)}) %all-to-all-start) | async-done | bytes 5242912 | tf_op jit(solution)/shard_map/all_to_all | solution.py:257
  149.5 5.5 %all-to-all-start.3 = ((bf16[128,40,512]{2,1,0:T(8,128)(2,1)}), bf16[128,40,512]{2,1,0:T(8,128)(2,1)}, u32[]{:S(2)}, u32[]{:S(2)}) async-start(bf16[128,40,512]{2,1,0:T(8,128)(2,1)} %bitcast.13), calls=%async_computation.3 | async-start | bytes 10485760 | tf_op jit(solution)/shard_map/all_to_all | solution.py:257
  155.1 28.5 %run_expert.2 = bf16[5120,512]{1,0:T(8,128)(2,1)} custom-call(s32[1]{0:T(128)S(6)} %add.3.limit_ref, bf16[5120,512]{1,0:T(8,128)(2,1)} %bitcast.4.in_ref, bf16[1,2048,768]{2,1,0:T(8,128)(2,1)} %gate_ref.3, bf16[1,2048,768]{2,1,0:T(8,128)(2,1)} %up_ref.3, bf16[1,768,2048]{2,1,0:T(8,128)(2,1)} %down_ref.3), custom_call_target="tpu_custom_call" | custom-call | tf_op jit(solution)/shard_map/run_expert/pallas_call | solution.py:233
  183.6 35.4 %all-to-all-done.3 = bf16[128,40,512]{2,1,0:T(8,128)(2,1)} async-done(((bf16[128,40,512]{2,1,0:T(8,128)(2,1)}), bf16[128,40,512]{2,1,0:T(8,128)(2,1)}, u32[]{:S(2)}, u32[]{:S(2)}) %all-to-all-start.3) | async-done | bytes 5242912 | tf_op jit(solution)/shard_map/all_to_all | solution.py:257
  219.0 5.5 %all-to-all-start.1 = ((bf16[128,40,512]{2,1,0:T(8,128)(2,1)}), bf16[128,40,512]{2,1,0:T(8,128)(2,1)}, u32[]{:S(2)}, u32[]{:S(2)}) async-start(bf16[128,40,512]{2,1,0:T(8,128)(2,1)} %bitcast.14), calls=%async_computation.1 | async-start | bytes 10485760 | tf_op jit(solution)/shard_map/all_to_all | solution.py:257
  224.6 4.0 %mix_answers.2.rest_0_ = bf16[2,128,2048]{2,1,0:T(8,128)(2,1)} custom-call(s32[2,8,128]{2,1,0:T(8,128)} %bitcast.17, f32[2,8,128]{2,1,0:T(8,128)} %bitcast.19, bf16[128,5,8,512]{3,2,1,0:T(8,128)(2,1)} %bitcast.10.rows_ref), custom_call_target="tpu_custom_call" | custom-call | tf_op jit(solution)/shard_map/mix_answers/pallas_call | solution.py:152
  228.6 60.0 %all-to-all-done.1 = bf16[128,40,512]{2,1,0:T(8,128)(2,1)} async-done(((bf16[128,40,512]{2,1,0:T(8,128)(2,1)}), bf16[128,40,512]{2,1,0:T(8,128)(2,1)}, u32[]{:S(2)}, u32[]{:S(2)}) %all-to-all-start.1) | async-done | bytes 5242912 | tf_op jit(solution)/shard_map/all_to_all | solution.py:257
  288.5 4.0 %mix_answers.3 = bf16[2,128,2048]{2,1,0:T(8,128)(2,1)} custom-call(s32[2,8,128]{2,1,0:T(8,128)} %bitcast.18, f32[2,8,128]{2,1,0:T(8,128)} %bitcast.20, bf16[128,5,8,512]{3,2,1,0:T(8,128)(2,1)} %bitcast.6.rows_ref, bf16[2,128,2048]{2,1,0:T(8,128)(2,1)} %mix_answers.2.rest_0_), custom_call_target="tpu_custom_call", output_to_operand_aliasing={{}: (3, {})} | custom-call | tf_op jit(solution)/shard_map/mix_answers/pallas_call | solution.py:152
Async XLA Ops:
  4.2 75.7 %all-to-all-start.2 = ((bf16[128,40,512]{2,1,0:T(8,128)(2,1)}), bf16[128,40,512]{2,1,0:T(8,128)(2,1)}, u32[]{:S(2)}, u32[]{:S(2)}) async-start(bf16[128,40,512]{2,1,0:T(8,128)(2,1)} %bitcast.12), calls=%async_computation.2 | async-start | bytes 10485760 | tf_op jit(solution)/shard_map/all_to_all | solution.py:257
  79.9 6.3 %copy-start = (s32[1,3]{1,0:T(1,128)S(1)}, s32[1,3]{1,0:T(1,128)}, u32[]{:S(2)}) copy-start(s32[1,3]{1,0:T(1,128)} %param.12) | copy-start | bytes 40
  79.9 69.6 %all-to-all-start = ((bf16[128,40,512]{2,1,0:T(8,128)(2,1)}), bf16[128,40,512]{2,1,0:T(8,128)(2,1)}, u32[]{:S(2)}, u32[]{:S(2)}) async-start(bf16[128,40,512]{2,1,0:T(8,128)(2,1)} %bitcast.11), calls=%async_computation | async-start | bytes 10485760 | tf_op jit(solution)/shard_map/all_to_all | solution.py:257
  149.5 69.5 %all-to-all-start.3 = ((bf16[128,40,512]{2,1,0:T(8,128)(2,1)}), bf16[128,40,512]{2,1,0:T(8,128)(2,1)}, u32[]{:S(2)}, u32[]{:S(2)}) async-start(bf16[128,40,512]{2,1,0:T(8,128)(2,1)} %bitcast.13), calls=%async_computation.3 | async-start | bytes 10485760 | tf_op jit(solution)/shard_map/all_to_all | solution.py:257
  219.0 69.5 %all-to-all-start.1 = ((bf16[128,40,512]{2,1,0:T(8,128)(2,1)}), bf16[128,40,512]{2,1,0:T(8,128)(2,1)}, u32[]{:S(2)}, u32[]{:S(2)}) async-start(bf16[128,40,512]{2,1,0:T(8,128)(2,1)} %bitcast.14), calls=%async_computation.1 | async-start | bytes 10485760 | tf_op jit(solution)/shard_map/all_to_all | solution.py:257

commit v4 on v3

--- a/solution.py
+++ b/solution.py
@@ -98,72 +98,59 @@
     )(ids, tokens)
 
 
-def mix_answers(answered, ids, probs, micro, earlier_out):
+def mix_answers(answered, ids, probs):
     micros, top, tok = ids.shape
     experts = lax.axis_size(AXES)
-    part = answered.shape[3]
+    part = answered[0].shape[3]
     width = part * PIECES
     rows = experts * TILE
 
-    def kernel(ids_ref, probs_ref, rows_ref, *rest):
-        out_ref, here_ref, my_ids_ref, my_probs_ref, sems = rest[-5:]
-
-        def fetch(q):
-            return pltpu.make_async_copy(rows_ref.at[:, q], here_ref.at[q], sems.at[q])
-
-        get_ids = pltpu.make_async_copy(ids_ref.at[micro], my_ids_ref, sems.at[PIECES + 1])
-        get_probs = pltpu.make_async_copy(probs_ref.at[micro], my_probs_ref, sems.at[PIECES + 2])
-        get_ids.start()
-        get_probs.start()
-        for q in (PIECES, *range(PIECES)):
-            fetch(q).start()
-        get_ids.wait()
-        get_probs.wait()
-        ids_here = my_ids_ref[...]
-        probs_here = my_probs_ref[...]
-        norm = probs_here / jnp.sum(probs_here, axis=0, keepdims=True)
+    def kernel(ids_ref, probs_ref, *rest):
+        rows_refs = rest[:micros]
+        out_ref, here_ref, sems = rest[micros:]
+
+        def fetch(m, q):
+            return pltpu.make_async_copy(rows_refs[m].at[:, q], here_ref.at[m, q], sems.at[m, q])
+
+        for m in range(micros):
+            for q in (PIECES, *range(PIECES)):
+                fetch(m, q).start()
         expert = iota((experts, tok), 0)
-        gate = jnp.zeros((experts, tok), jnp.float32)
-        for k in range(top):
-            gate = jnp.where(ids_here[k : k + 1, :] == expert, norm[k : k + 1, :], gate)
         spread = narrow(bit((iota((experts, rows), 1) >> 3) == iota((experts, rows), 0)))
-        rank = mm(narrow(chosen_rank(ids_here, experts).T), spread)
-        gate = mm(narrow(gate.T), spread)
         inside = iota((tok, rows), 1) & 7
-        weight = narrow(jnp.where(rank == (inside + 1).astype(jnp.float32), gate, 0.0))
-        rest_weight = jnp.where(rank == ((inside >> 2) + (TILE + 1)).astype(jnp.float32), gate, 0.0)
-        rest_weight = jnp.concatenate(
-            [narrow(jnp.where((inside & 3) == q, rest_weight, 0.0)) for q in range(PIECES)], axis=0
-        )
-        fetch(PIECES).wait()
-        last = mm(rest_weight, here_ref[PIECES].reshape(rows, part))
-        for q in range(PIECES):
-            fetch(q).wait()
-            main = mm(weight, here_ref[q].reshape(rows, part))
-            out_ref[0, :, q * part : (q + 1) * part] = narrow(main + last[q * tok : (q + 1) * tok])
-
-    in_specs = [pl.BlockSpec(memory_space=pl.ANY)] * 3
-    operands = [ids, probs, answered]
-    aliases = {}
-    if earlier_out is not None:
-        in_specs.append(pl.BlockSpec(memory_space=pl.ANY))
-        operands.append(earlier_out)
-        aliases = {3: 0}
+        for m in range(micros):
+            ids_here = ids_ref[m]
+            norm = probs_ref[m] / jnp.sum(probs_ref[m], axis=0, keepdims=True)
+            gate = jnp.zeros((experts, tok), jnp.float32)
+            for k in range(top):
+                gate = jnp.where(ids_here[k : k + 1, :] == expert, norm[k : k + 1, :], gate)
+            rank = mm(narrow(chosen_rank(ids_here, experts).T), spread)
+            gate = mm(narrow(gate.T), spread)
+            weight = narrow(jnp.where(rank == (inside + 1).astype(jnp.float32), gate, 0.0))
+            rest_weight = jnp.where(rank == ((inside >> 2) + (TILE + 1)).astype(jnp.float32), gate, 0.0)
+            rest_weight = jnp.concatenate(
+                [narrow(jnp.where((inside & 3) == q, rest_weight, 0.0)) for q in range(PIECES)], axis=0
+            )
+            fetch(m, PIECES).wait()
+            last = mm(rest_weight, here_ref[m, PIECES].reshape(rows, part))
+            for q in range(PIECES):
+                fetch(m, q).wait()
+                main = mm(weight, here_ref[m, q].reshape(rows, part))
+                out_ref[m, :, q * part : (q + 1) * part] = narrow(main + last[q * tok : (q + 1) * tok])
+
+    whole = pl.BlockSpec((micros, top, tok), lambda i: (0, 0, 0))
     return pl.pallas_call(
         kernel,
         grid=(1,),
-        in_specs=in_specs,
-        out_specs=pl.BlockSpec((1, tok, width), lambda i: (micro, 0, 0)),
+        in_specs=[whole, whole] + [pl.BlockSpec(memory_space=pl.ANY)] * micros,
+        out_specs=pl.BlockSpec((micros, tok, width), lambda i: (0, 0, 0)),
         out_shape=jax.ShapeDtypeStruct((micros, tok, width), jnp.bfloat16),
         scratch_shapes=[
-            pltpu.VMEM((PIECES + 1, experts, TILE, part), jnp.bfloat16),
-            pltpu.VMEM((top, tok), ids.dtype),
-            pltpu.VMEM((top, tok), probs.dtype),
-            pltpu.SemaphoreType.DMA((PIECES + 3,)),
-        ],
-        input_output_aliases=aliases,
+            pltpu.VMEM((micros, PIECES + 1, experts, TILE, part), jnp.bfloat16),
+            pltpu.SemaphoreType.DMA((micros, PIECES + 1)),
+        ],
         name="mix_answers",
-    )(*operands)
+    )(ids, probs, *answered)
 
 
 def place(row, slots, q):
@@ -276,11 +263,8 @@
         incoming = arrived[m].reshape(-1, width // PIECES)
         returned = run_expert(incoming, keep_limit, w_gate, w_up, w_down, slots, block_devices)
         answers.append(swap(returned, devices))
-    out = None
-    for m in range(micros):
-        answered = answers[m].reshape(devices, PIECES + 1, TILE, width // PIECES)
-        out = mix_answers(answered, ids, probs, m, out)
-    return out
+    answered = [a.reshape(devices, PIECES + 1, TILE, width // PIECES) for a in answers]
+    return mix_answers(answered, ids, probs)
 
 
 def solution(mesh):

time: 293 us -> 296 us (1.010)
  blocking collectives: 0 us -> 69.8 us
  waiting for transfers between devices: 189 us -> 129 us
  starting transfers between devices: 28.6 us -> 23.1 us
    all_to_all x0 -> x1, blocking collectives: none -> 69.8 us  [swap(): return lax.all_to_all(parts, AXES, split_axis=0, concat_axis=0, tiled=True)]
    all_to_all x4 -> x3, waiting for transfers between devices: 189 us -> 129 us  [swap(): return lax.all_to_all(parts, AXES, split_axis=0, concat_axis=0, tiled=True)]
    all_to_all x4 -> x3, starting transfers between devices: 28.6 us -> 23.1 us  [swap(): return lax.all_to_all(parts, AXES, split_axis=0, concat_axis=0, tiled=True)]
    pallas_call x2 -> x1, Pallas kernels: 7.94 us -> 7.06 us  [mix_answers(): pl.pallas_call(kernel, grid=(1,), in_specs=[whole, whole] + [pl.BlockSpec...]
  transfers between devices with their start and end apart: 4 -> 3, of which waited for: 4 -> 3; matrix products, arithmetic and copies ran while one was open for 0% -> 0% of each run, Pallas kernels for 22% -> 21%
where the time goes in v4:
time: 296 us
  waiting for transfers between devices  129 us (44%)
  Pallas kernels  72.3 us (24%)
  blocking collectives  69.8 us (24%)
  starting transfers between devices  23.1 us (8%)
    all_to_all x3, waiting for transfers between devices, swap(): return lax.all_to_all(parts, AXES, split_axis=0, concat_axis=0, tiled=True)  129 us
    all_to_all x1, blocking collectives, swap(): return lax.all_to_all(parts, AXES, split_axis=0, concat_axis=0, tiled=True)  69.8 us
    pallas_call x2, Pallas kernels, run_expert(): pl.pallas_call(kernel, grid=(steps,), in_specs=[pl.BlockSpec(memory_space...  57.1 us
    all_to_all x3, starting transfers between devices, swap(): return lax.all_to_all(parts, AXES, split_axis=0, concat_axis=0, tiled=True)  23.1 us
    pallas_call x2, Pallas kernels, pack_tokens(): pl.pallas_call(kernel, grid=(1,), in_specs=[pl.BlockSpec(memory_space=pl....  8.18 us
    pallas_call x1, Pallas kernels, mix_answers(): pl.pallas_call(kernel, grid=(1,), in_specs=[whole, whole] + [pl.BlockSpec...  7.06 us
  transfers between devices with their start and end apart: 3, of which 3 were waited for; matrix products, arithmetic and copies ran while one was open for 0% of the time, Pallas kernels for 21%

profile of v4, /device:TPU:1, one launch (start us, length us, event | category | flops | bytes accessed | tf_op | source)
XLA Modules:
  0.0 295.9 jit_solution(5304483639953278885)
XLA Ops:
  0.0 4.1 %pack_tokens.3 = bf16[128,5,8,512]{3,2,1,0:T(8,128)(2,1)} custom-call(s32[2,8,128]{2,1,0:T(8,128)} %bitcast.16, bf16[2,128,2048]{2,1,0:T(8,128)(2,1)} %tok_ref.3), custom_call_target="tpu_custom_call" | custom-call | tf_op jit(solution)/shard_map/pack_tokens/pallas_call | solution.py:85
  4.1 11.9 %all-to-all-start.2 = ((bf16[128,40,512]{2,1,0:T(8,128)(2,1)}), bf16[128,40,512]{2,1,0:T(8,128)(2,1)}, u32[]{:S(2)}, u32[]{:S(2)}) async-start(bf16[128,40,512]{2,1,0:T(8,128)(2,1)} %bitcast.12), calls=%async_computation.2 | async-start | bytes 10485760 | tf_op jit(solution)/shard_map/all_to_all | solution.py:244
  16.0 4.1 %pack_tokens.2 = bf16[128,5,8,512]{3,2,1,0:T(8,128)(2,1)} custom-call(s32[2,8,128]{2,1,0:T(8,128)} %bitcast.17, bf16[2,128,2048]{2,1,0:T(8,128)(2,1)} %tok_ref.3), custom_call_target="tpu_custom_call" | custom-call | tf_op jit(solution)/shard_map/pack_tokens/pallas_call | solution.py:85
  20.1 59.7 %all-to-all-done.2 = bf16[128,40,512]{2,1,0:T(8,128)(2,1)} async-done(((bf16[128,40,512]{2,1,0:T(8,128)(2,1)}), bf16[128,40,512]{2,1,0:T(8,128)(2,1)}, u32[]{:S(2)}, u32[]{:S(2)}) %all-to-all-start.2) | async-done | bytes 5242912 | tf_op jit(solution)/shard_map/all_to_all | solution.py:244
  79.8 0.0 copy-start
  79.8 5.7 %all-to-all-start = ((bf16[128,40,512]{2,1,0:T(8,128)(2,1)}), bf16[128,40,512]{2,1,0:T(8,128)(2,1)}, u32[]{:S(2)}, u32[]{:S(2)}) async-start(bf16[128,40,512]{2,1,0:T(8,128)(2,1)} %bitcast.11), calls=%async_computation | async-start | bytes 10485760 | tf_op jit(solution)/shard_map/all_to_all | solution.py:244
  86.1 0.0 copy-done
  86.1 0.6 reduce_sum.11
  87.4 28.5 %run_expert.3 = bf16[5120,512]{1,0:T(8,128)(2,1)} custom-call(s32[1]{0:T(128)S(6)} %add.3.limit_ref, bf16[5120,512]{1,0:T(8,128)(2,1)} %bitcast.8.in_ref, bf16[1,2048,768]{2,1,0:T(8,128)(2,1)} %gate_ref.3, bf16[1,2048,768]{2,1,0:T(8,128)(2,1)} %up_ref.3, bf16[1,768,2048]{2,1,0:T(8,128)(2,1)} %down_ref.3), custom_call_target="tpu_custom_call" | custom-call | tf_op jit(solution)/shard_map/run_expert/pallas_call | solution.py:220
  116.0 33.5 %all-to-all-done = bf16[128,40,512]{2,1,0:T(8,128)(2,1)} async-done(((bf16[128,40,512]{2,1,0:T(8,128)(2,1)}), bf16[128,40,512]{2,1,0:T(8,128)(2,1)}, u32[]{:S(2)}, u32[]{:S(2)}) %all-to-all-start) | async-done | bytes 5242912 | tf_op jit(solution)/shard_map/all_to_all | solution.py:244
  149.4 5.5 %all-to-all-start.3 = ((bf16[128,40,512]{2,1,0:T(8,128)(2,1)}), bf16[128,40,512]{2,1,0:T(8,128)(2,1)}, u32[]{:S(2)}, u32[]{:S(2)}) async-start(bf16[128,40,512]{2,1,0:T(8,128)(2,1)} %bitcast.14), calls=%async_computation.3 | async-start | bytes 10485760 | tf_op jit(solution)/shard_map/all_to_all | solution.py:244
  155.0 28.5 %run_expert.2 = bf16[5120,512]{1,0:T(8,128)(2,1)} custom-call(s32[1]{0:T(128)S(6)} %add.3.limit_ref, bf16[5120,512]{1,0:T(8,128)(2,1)} %bitcast.4.in_ref, bf16[1,2048,768]{2,1,0:T(8,128)(2,1)} %gate_ref.3, bf16[1,2048,768]{2,1,0:T(8,128)(2,1)} %up_ref.3, bf16[1,768,2048]{2,1,0:T(8,128)(2,1)} %down_ref.3), custom_call_target="tpu_custom_call" | custom-call | tf_op jit(solution)/shard_map/run_expert/pallas_call | solution.py:220
  183.5 35.4 %all-to-all-done.3 = bf16[128,40,512]{2,1,0:T(8,128)(2,1)} async-done(((bf16[128,40,512]{2,1,0:T(8,128)(2,1)}), bf16[128,40,512]{2,1,0:T(8,128)(2,1)}, u32[]{:S(2)}, u32[]{:S(2)}) %all-to-all-start.3) | async-done | bytes 5242912 | tf_op jit(solution)/shard_map/all_to_all | solution.py:244
  218.9 69.8 %all_to_all.20 = bf16[128,40,512]{2,1,0:T(8,128)(2,1)} all-to-all(bf16[128,40,512]{2,1,0:T(8,128)(2,1)} %bitcast.15), channel_id=1, replica_groups=mesh['expert'=16,'group'=8] {'expert','group'}, dimensions={0} | all-to-all | bytes 10485760 | tf_op jit(solution)/shard_map/all_to_all | solution.py:244
  288.7 7.1 %mix_answers.1 = bf16[2,128,2048]{2,1,0:T(8,128)(2,1)} custom-call(s32[2,8,128]{2,1,0:T(8,128)} %bitcast.18, f32[2,8,128]{2,1,0:T(8,128)} %bitcast.19, bf16[128,5,8,512]{3,2,1,0:T(8,128)(2,1)} %bitcast.13, bf16[128,5,8,512]{3,2,1,0:T(8,128)(2,1)} %bitcast.10.rest_1_), custom_call_target="tpu_custom_call" | custom-call | tf_op jit(solution)/shard_map/mix_answers/pallas_call | solution.py:142
Async XLA Ops:
  4.1 75.7 %all-to-all-start.2 = ((bf16[128,40,512]{2,1,0:T(8,128)(2,1)}), bf16[128,40,512]{2,1,0:T(8,128)(2,1)}, u32[]{:S(2)}, u32[]{:S(2)}) async-start(bf16[128,40,512]{2,1,0:T(8,128)(2,1)} %bitcast.12), calls=%async_computation.2 | async-start | bytes 10485760 | tf_op jit(solution)/shard_map/all_to_all | solution.py:244
  79.8 6.3 %copy-start = (s32[1,3]{1,0:T(1,128)S(1)}, s32[1,3]{1,0:T(1,128)}, u32[]{:S(2)}) copy-start(s32[1,3]{1,0:T(1,128)} %param.12) | copy-start | bytes 40
  79.8 69.6 %all-to-all-start = ((bf16[128,40,512]{2,1,0:T(8,128)(2,1)}), bf16[128,40,512]{2,1,0:T(8,128)(2,1)}, u32[]{:S(2)}, u32[]{:S(2)}) async-start(bf16[128,40,512]{2,1,0:T(8,128)(2,1)} %bitcast.11), calls=%async_computation | async-start | bytes 10485760 | tf_op jit(solution)/shard_map/all_to_all | solution.py:244
  149.4 69.5 %all-to-all-start.3 = ((bf16[128,40,512]{2,1,0:T(8,128)(2,1)}), bf16[128,40,512]{2,1,0:T(8,128)(2,1)}, u32[]{:S(2)}, u32[]{:S(2)}) async-start(bf16[128,40,512]{2,1,0:T(8,128)(2,1)} %bitcast.14), calls=%async_computation.3 | async-start | bytes 10485760 | tf_op jit(solution)/shard_map/all_to_all | solution.py:244

commit v5 on v3

--- a/solution.py
+++ b/solution.py
@@ -106,7 +106,11 @@
     rows = experts * TILE
 
     def kernel(ids_ref, probs_ref, rows_ref, *rest):
-        out_ref, here_ref, my_ids_ref, my_probs_ref, sems = rest[-5:]
+        out_ref, here_ref, my_ids_ref, my_probs_ref, sum_ref, sems = rest[-6:]
+
+        def leave(q):
+            columns = out_ref.at[micro, :, pl.ds(q * part, part)]
+            return pltpu.make_async_copy(sum_ref.at[q], columns, sems.at[PIECES + 3 + q])
 
         def fetch(q):
             return pltpu.make_async_copy(rows_ref.at[:, q], here_ref.at[q], sems.at[q])
@@ -140,7 +144,10 @@
         for q in range(PIECES):
             fetch(q).wait()
             main = mm(weight, here_ref[q].reshape(rows, part))
-            out_ref[0, :, q * part : (q + 1) * part] = narrow(main + last[q * tok : (q + 1) * tok])
+            sum_ref[q] = narrow(main + last[q * tok : (q + 1) * tok])
+            leave(q).start()
+        for q in range(PIECES):
+            leave(q).wait()
 
     in_specs = [pl.BlockSpec(memory_space=pl.ANY)] * 3
     operands = [ids, probs, answered]
@@ -153,13 +160,14 @@
         kernel,
         grid=(1,),
         in_specs=in_specs,
-        out_specs=pl.BlockSpec((1, tok, width), lambda i: (micro, 0, 0)),
+        out_specs=pl.BlockSpec(memory_space=pl.ANY),
         out_shape=jax.ShapeDtypeStruct((micros, tok, width), jnp.bfloat16),
         scratch_shapes=[
             pltpu.VMEM((PIECES + 1, experts, TILE, part), jnp.bfloat16),
             pltpu.VMEM((top, tok), ids.dtype),
             pltpu.VMEM((top, tok), probs.dtype),
-            pltpu.SemaphoreType.DMA((PIECES + 3,)),
+            pltpu.VMEM((PIECES, tok, part), jnp.bfloat16),
+            pltpu.SemaphoreType.DMA((2 * PIECES + 3,)),
         ],
         input_output_aliases=aliases,
         name="mix_answers",

time: 293 us -> 293 us (level)
  no operation moved by 1% of the time
where the time goes in v5:
time: 293 us
  waiting for transfers between devices  189 us (65%)
  Pallas kernels  73.1 us (25%)
  starting transfers between devices  28.6 us (10%)
    all_to_all x4, waiting for transfers between devices, swap(): return lax.all_to_all(parts, AXES, split_axis=0, concat_axis=0, tiled=True)  189 us
    pallas_call x2, Pallas kernels, run_expert(): pl.pallas_call(kernel, grid=(steps,), in_specs=[pl.BlockSpec(memory_space...  57.1 us
    all_to_all x4, starting transfers between devices, swap(): return lax.all_to_all(parts, AXES, split_axis=0, concat_axis=0, tiled=True)  28.6 us
    pallas_call x2, Pallas kernels, pack_tokens(): pl.pallas_call(kernel, grid=(1,), in_specs=[pl.BlockSpec(memory_space=pl....  8.28 us
    pallas_call x2, Pallas kernels, mix_answers(): pl.pallas_call(kernel, grid=(1,), in_specs=in_specs, out_specs=pl.BlockSp...  7.74 us
  transfers between devices with their start and end apart: 4, of which 4 were waited for; matrix products, arithmetic and copies ran while one was open for 0% of the time, Pallas kernels for 22%

profile of v5, /device:TPU:1, one launch (start us, length us, event | category | flops | bytes accessed | tf_op | source)
XLA Modules:
  0.0 292.6 jit_solution(17376510010719970569)
XLA Ops:
  0.0 4.2 %pack_tokens.3 = bf16[128,5,8,512]{3,2,1,0:T(8,128)(2,1)} custom-call(s32[2,8,128]{2,1,0:T(8,128)} %bitcast.15, bf16[2,128,2048]{2,1,0:T(8,128)(2,1)} %tok_ref.3), custom_call_target="tpu_custom_call" | custom-call | tf_op jit(solution)/shard_map/pack_tokens/pallas_call | solution.py:85
  4.2 11.9 %all-to-all-start.2 = ((bf16[128,40,512]{2,1,0:T(8,128)(2,1)}), bf16[128,40,512]{2,1,0:T(8,128)(2,1)}, u32[]{:S(2)}, u32[]{:S(2)}) async-start(bf16[128,40,512]{2,1,0:T(8,128)(2,1)} %bitcast.12), calls=%async_computation.2 | async-start | bytes 10485760 | tf_op jit(solution)/shard_map/all_to_all | solution.py:265
  16.1 4.1 %pack_tokens.2 = bf16[128,5,8,512]{3,2,1,0:T(8,128)(2,1)} custom-call(s32[2,8,128]{2,1,0:T(8,128)} %bitcast.16, bf16[2,128,2048]{2,1,0:T(8,128)(2,1)} %tok_ref.3), custom_call_target="tpu_custom_call" | custom-call | tf_op jit(solution)/shard_map/pack_tokens/pallas_call | solution.py:85
  20.2 59.7 %all-to-all-done.2 = bf16[128,40,512]{2,1,0:T(8,128)(2,1)} async-done(((bf16[128,40,512]{2,1,0:T(8,128)(2,1)}), bf16[128,40,512]{2,1,0:T(8,128)(2,1)}, u32[]{:S(2)}, u32[]{:S(2)}) %all-to-all-start.2) | async-done | bytes 5242912 | tf_op jit(solution)/shard_map/all_to_all | solution.py:265
  79.9 0.0 copy-start
  79.9 5.7 %all-to-all-start = ((bf16[128,40,512]{2,1,0:T(8,128)(2,1)}), bf16[128,40,512]{2,1,0:T(8,128)(2,1)}, u32[]{:S(2)}, u32[]{:S(2)}) async-start(bf16[128,40,512]{2,1,0:T(8,128)(2,1)} %bitcast.11), calls=%async_computation | async-start | bytes 10485760 | tf_op jit(solution)/shard_map/all_to_all | solution.py:265
  86.2 0.0 copy-done
  86.2 0.6 reduce_sum.11
  87.5 28.5 %run_expert.3 = bf16[5120,512]{1,0:T(8,128)(2,1)} custom-call(s32[1]{0:T(128)S(6)} %add.3.limit_ref, bf16[5120,512]{1,0:T(8,128)(2,1)} %bitcast.8.in_ref, bf16[1,2048,768]{2,1,0:T(8,128)(2,1)} %gate_ref.3, bf16[1,2048,768]{2,1,0:T(8,128)(2,1)} %up_ref.3, bf16[1,768,2048]{2,1,0:T(8,128)(2,1)} %down_ref.3), custom_call_target="tpu_custom_call" | custom-call | tf_op jit(solution)/shard_map/run_expert/pallas_call | solution.py:241
  116.0 33.5 %all-to-all-done = bf16[128,40,512]{2,1,0:T(8,128)(2,1)} async-done(((bf16[128,40,512]{2,1,0:T(8,128)(2,1)}), bf16[128,40,512]{2,1,0:T(8,128)(2,1)}, u32[]{:S(2)}, u32[]{:S(2)}) %all-to-all-start) | async-done | bytes 5242912 | tf_op jit(solution)/shard_map/all_to_all | solution.py:265
  149.5 5.5 %all-to-all-start.3 = ((bf16[128,40,512]{2,1,0:T(8,128)(2,1)}), bf16[128,40,512]{2,1,0:T(8,128)(2,1)}, u32[]{:S(2)}, u32[]{:S(2)}) async-start(bf16[128,40,512]{2,1,0:T(8,128)(2,1)} %bitcast.13), calls=%async_computation.3 | async-start | bytes 10485760 | tf_op jit(solution)/shard_map/all_to_all | solution.py:265
  155.1 28.5 %run_expert.2 = bf16[5120,512]{1,0:T(8,128)(2,1)} custom-call(s32[1]{0:T(128)S(6)} %add.3.limit_ref, bf16[5120,512]{1,0:T(8,128)(2,1)} %bitcast.4.in_ref, bf16[1,2048,768]{2,1,0:T(8,128)(2,1)} %gate_ref.3, bf16[1,2048,768]{2,1,0:T(8,128)(2,1)} %up_ref.3, bf16[1,768,2048]{2,1,0:T(8,128)(2,1)} %down_ref.3), custom_call_target="tpu_custom_call" | custom-call | tf_op jit(solution)/shard_map/run_expert/pallas_call | solution.py:241
  183.6 35.4 %all-to-all-done.3 = bf16[128,40,512]{2,1,0:T(8,128)(2,1)} async-done(((bf16[128,40,512]{2,1,0:T(8,128)(2,1)}), bf16[128,40,512]{2,1,0:T(8,128)(2,1)}, u32[]{:S(2)}, u32[]{:S(2)}) %all-to-all-start.3) | async-done | bytes 5242912 | tf_op jit(solution)/shard_map/all_to_all | solution.py:265
  219.0 5.5 %all-to-all-start.1 = ((bf16[128,40,512]{2,1,0:T(8,128)(2,1)}), bf16[128,40,512]{2,1,0:T(8,128)(2,1)}, u32[]{:S(2)}, u32[]{:S(2)}) async-start(bf16[128,40,512]{2,1,0:T(8,128)(2,1)} %bitcast.14), calls=%async_computation.1 | async-start | bytes 10485760 | tf_op jit(solution)/shard_map/all_to_all | solution.py:265
  224.6 3.9 %mix_answers.2.rest_0_ = bf16[2,128,2048]{2,1,0:T(8,128)(2,1)} custom-call(s32[2,8,128]{2,1,0:T(8,128)} %bitcast.17, f32[2,8,128]{2,1,0:T(8,128)} %bitcast.19, bf16[128,5,8,512]{3,2,1,0:T(8,128)(2,1)} %bitcast.10.rows_ref), custom_call_target="tpu_custom_call" | custom-call | tf_op jit(solution)/shard_map/mix_answers/pallas_call | solution.py:159
  228.5 60.1 %all-to-all-done.1 = bf16[128,40,512]{2,1,0:T(8,128)(2,1)} async-done(((bf16[128,40,512]{2,1,0:T(8,128)(2,1)}), bf16[128,40,512]{2,1,0:T(8,128)(2,1)}, u32[]{:S(2)}, u32[]{:S(2)}) %all-to-all-start.1) | async-done | bytes 5242912 | tf_op jit(solution)/shard_map/all_to_all | solution.py:265
  288.5 3.9 %mix_answers.3 = bf16[2,128,2048]{2,1,0:T(8,128)(2,1)} custom-call(s32[2,8,128]{2,1,0:T(8,128)} %bitcast.18, f32[2,8,128]{2,1,0:T(8,128)} %bitcast.20, bf16[128,5,8,512]{3,2,1,0:T(8,128)(2,1)} %bitcast.6.rows_ref, bf16[2,128,2048]{2,1,0:T(8,128)(2,1)} %mix_answers.2.rest_0_), custom_call_target="tpu_custom_call", output_to_operand_aliasing={{}: (3, {})} | custom-call | tf_op jit(solution)/shard_map/mix_answers/pallas_call | solution.py:159
Async XLA Ops:
  4.2 75.7 %all-to-all-start.2 = ((bf16[128,40,512]{2,1,0:T(8,128)(2,1)}), bf16[128,40,512]{2,1,0:T(8,128)(2,1)}, u32[]{:S(2)}, u32[]{:S(2)}) async-start(bf16[128,40,512]{2,1,0:T(8,128)(2,1)} %bitcast.12), calls=%async_computation.2 | async-start | bytes 10485760 | tf_op jit(solution)/shard_map/all_to_all | solution.py:265
  79.9 6.3 %copy-start = (s32[1,3]{1,0:T(1,128)S(1)}, s32[1,3]{1,0:T(1,128)}, u32[]{:S(2)}) copy-start(s32[1,3]{1,0:T(1,128)} %param.12) | copy-start | bytes 40
  79.9 69.6 %all-to-all-start = ((bf16[128,40,512]{2,1,0:T(8,128)(2,1)}), bf16[128,40,512]{2,1,0:T(8,128)(2,1)}, u32[]{:S(2)}, u32[]{:S(2)}) async-start(bf16[128,40,512]{2,1,0:T(8,128)(2,1)} %bitcast.11), calls=%async_computation | async-start | bytes 10485760 | tf_op jit(solution)/shard_map/all_to_all | solution.py:265
  149.5 69.5 %all-to-all-start.3 = ((bf16[128,40,512]{2,1,0:T(8,128)(2,1)}), bf16[128,40,512]{2,1,0:T(8,128)(2,1)}, u32[]{:S(2)}, u32[]{:S(2)}) async-start(bf16[128,40,512]{2,1,0:T(8,128)(2,1)} %bitcast.13), calls=%async_computation.3 | async-start | bytes 10485760 | tf_op jit(solution)/shard_map/all_to_all | solution.py:265
  219.0 69.5 %all-to-all-start.1 = ((bf16[128,40,512]{2,1,0:T(8,128)(2,1)}), bf16[128,40,512]{2,1,0:T(8,128)(2,1)}, u32[]{:S(2)}, u32[]{:S(2)}) async-start(bf16[128,40,512]{2,1,0:T(8,128)(2,1)} %bitcast.14), calls=%async_computation.1 | async-start | bytes 10485760 | tf_op jit(solution)/shard_map/all_to_all | solution.py:265

commit v6 on v5

--- a/solution.py
+++ b/solution.py
@@ -62,11 +62,11 @@
         hit = bit(rank == (inside + 1).astype(jnp.float32))
         select = narrow(hit)
         first = col == 0
-        mark = jnp.where((jnp.sum(hit, axis=1, keepdims=True) < 0.5) & first, MARK, 0.0)
         get_tokens.wait()
-        for q in range(PIECES):
+        for q in (*range(1, PIECES), 0):
             moved = mm(select, my_tok_ref[:, q * part : (q + 1) * part])
             if q == 0:
+                mark = jnp.where((jnp.sum(hit, axis=1, keepdims=True) < 0.5) & first, MARK, 0.0)
                 moved = jnp.concatenate([moved[:, :experts] + mark, moved[:, experts:]], axis=1)
             sent_ref[q] = narrow(moved.reshape(experts, TILE, part))
             leave(q).start()

time: 293 us -> 293 us (level)
  no operation moved by 1% of the time
where the time goes in v6:
time: 293 us; the launch traced here: 292 us
  waiting for transfers between devices  189 us (65%)
  Pallas kernels  72.8 us (25%)
  starting transfers between devices  28.6 us (10%)
    all_to_all x4, waiting for transfers between devices, swap(): return lax.all_to_all(parts, AXES, split_axis=0, concat_axis=0, tiled=True)  189 us
    pallas_call x2, Pallas kernels, run_expert(): pl.pallas_call(kernel, grid=(steps,), in_specs=[pl.BlockSpec(memory_space...  57.1 us
    all_to_all x4, starting transfers between devices, swap(): return lax.all_to_all(parts, AXES, split_axis=0, concat_axis=0, tiled=True)  28.6 us
    pallas_call x2, Pallas kernels, pack_tokens(): pl.pallas_call(kernel, grid=(1,), in_specs=[pl.BlockSpec(memory_space=pl....  8.04 us
    pallas_call x2, Pallas kernels, mix_answers(): pl.pallas_call(kernel, grid=(1,), in_specs=in_specs, out_specs=pl.BlockSp...  7.73 us
  transfers between devices with their start and end apart: 4, of which 4 were waited for; matrix products, arithmetic and copies ran while one was open for 0% of the time, Pallas kernels for 22%

profile of v6, /device:TPU:1, one launch (start us, length us, event | category | flops | bytes accessed | tf_op | source)
XLA Modules:
  0.0 292.4 jit_solution(12877266886014712401)
XLA Ops:
  0.0 4.0 %pack_tokens.3 = bf16[128,5,8,512]{3,2,1,0:T(8,128)(2,1)} custom-call(s32[2,8,128]{2,1,0:T(8,128)} %bitcast.15, bf16[2,128,2048]{2,1,0:T(8,128)(2,1)} %tok_ref.3), custom_call_target="tpu_custom_call" | custom-call | tf_op jit(solution)/shard_map/pack_tokens/pallas_call | solution.py:85
  4.1 11.9 %all-to-all-start.2 = ((bf16[128,40,512]{2,1,0:T(8,128)(2,1)}), bf16[128,40,512]{2,1,0:T(8,128)(2,1)}, u32[]{:S(2)}, u32[]{:S(2)}) async-start(bf16[128,40,512]{2,1,0:T(8,128)(2,1)} %bitcast.12), calls=%async_computation.2 | async-start | bytes 10485760 | tf_op jit(solution)/shard_map/all_to_all | solution.py:265
  16.0 4.0 %pack_tokens.2 = bf16[128,5,8,512]{3,2,1,0:T(8,128)(2,1)} custom-call(s32[2,8,128]{2,1,0:T(8,128)} %bitcast.16, bf16[2,128,2048]{2,1,0:T(8,128)(2,1)} %tok_ref.3), custom_call_target="tpu_custom_call" | custom-call | tf_op jit(solution)/shard_map/pack_tokens/pallas_call | solution.py:85
  20.0 59.8 %all-to-all-done.2 = bf16[128,40,512]{2,1,0:T(8,128)(2,1)} async-done(((bf16[128,40,512]{2,1,0:T(8,128)(2,1)}), bf16[128,40,512]{2,1,0:T(8,128)(2,1)}, u32[]{:S(2)}, u32[]{:S(2)}) %all-to-all-start.2) | async-done | bytes 5242912 | tf_op jit(solution)/shard_map/all_to_all | solution.py:265
  79.8 0.0 copy-start
  79.8 5.7 %all-to-all-start = ((bf16[128,40,512]{2,1,0:T(8,128)(2,1)}), bf16[128,40,512]{2,1,0:T(8,128)(2,1)}, u32[]{:S(2)}, u32[]{:S(2)}) async-start(bf16[128,40,512]{2,1,0:T(8,128)(2,1)} %bitcast.11), calls=%async_computation | async-start | bytes 10485760 | tf_op jit(solution)/shard_map/all_to_all | solution.py:265
  86.1 0.0 copy-done
  86.1 0.6 reduce_sum.11
  87.4 28.5 %run_expert.3 = bf16[5120,512]{1,0:T(8,128)(2,1)} custom-call(s32[1]{0:T(128)S(6)} %add.3.limit_ref, bf16[5120,512]{1,0:T(8,128)(2,1)} %bitcast.8.in_ref, bf16[1,2048,768]{2,1,0:T(8,128)(2,1)} %gate_ref.3, bf16[1,2048,768]{2,1,0:T(8,128)(2,1)} %up_ref.3, bf16[1,768,2048]{2,1,0:T(8,128)(2,1)} %down_ref.3), custom_call_target="tpu_custom_call" | custom-call | tf_op jit(solution)/shard_map/run_expert/pallas_call | solution.py:241
  115.9 33.5 %all-to-all-done = bf16[128,40,512]{2,1,0:T(8,128)(2,1)} async-done(((bf16[128,40,512]{2,1,0:T(8,128)(2,1)}), bf16[128,40,512]{2,1,0:T(8,128)(2,1)}, u32[]{:S(2)}, u32[]{:S(2)}) %all-to-all-start) | async-done | bytes 5242912 | tf_op jit(solution)/shard_map/all_to_all | solution.py:265
  149.4 5.5 %all-to-all-start.3 = ((bf16[128,40,512]{2,1,0:T(8,128)(2,1)}), bf16[128,40,512]{2,1,0:T(8,128)(2,1)}, u32[]{:S(2)}, u32[]{:S(2)}) async-start(bf16[128,40,512]{2,1,0:T(8,128)(2,1)} %bitcast.13), calls=%async_computation.3 | async-start | bytes 10485760 | tf_op jit(solution)/shard_map/all_to_all | solution.py:265
  155.0 28.5 %run_expert.2 = bf16[5120,512]{1,0:T(8,128)(2,1)} custom-call(s32[1]{0:T(128)S(6)} %add.3.limit_ref, bf16[5120,512]{1,0:T(8,128)(2,1)} %bitcast.4.in_ref, bf16[1,2048,768]{2,1,0:T(8,128)(2,1)} %gate_ref.3, bf16[1,2048,768]{2,1,0:T(8,128)(2,1)} %up_ref.3, bf16[1,768,2048]{2,1,0:T(8,128)(2,1)} %down_ref.3), custom_call_target="tpu_custom_call" | custom-call | tf_op jit(solution)/shard_map/run_expert/pallas_call | solution.py:241
  183.5 35.4 %all-to-all-done.3 = bf16[128,40,512]{2,1,0:T(8,128)(2,1)} async-done(((bf16[128,40,512]{2,1,0:T(8,128)(2,1)}), bf16[128,40,512]{2,1,0:T(8,128)(2,1)}, u32[]{:S(2)}, u32[]{:S(2)}) %all-to-all-start.3) | async-done | bytes 5242912 | tf_op jit(solution)/shard_map/all_to_all | solution.py:265
  218.9 5.5 %all-to-all-start.1 = ((bf16[128,40,512]{2,1,0:T(8,128)(2,1)}), bf16[128,40,512]{2,1,0:T(8,128)(2,1)}, u32[]{:S(2)}, u32[]{:S(2)}) async-start(bf16[128,40,512]{2,1,0:T(8,128)(2,1)} %bitcast.14), calls=%async_computation.1 | async-start | bytes 10485760 | tf_op jit(solution)/shard_map/all_to_all | solution.py:265
  224.5 3.9 %mix_answers.2.rest_0_ = bf16[2,128,2048]{2,1,0:T(8,128)(2,1)} custom-call(s32[2,8,128]{2,1,0:T(8,128)} %bitcast.17, f32[2,8,128]{2,1,0:T(8,128)} %bitcast.19, bf16[128,5,8,512]{3,2,1,0:T(8,128)(2,1)} %bitcast.10.rows_ref), custom_call_target="tpu_custom_call" | custom-call | tf_op jit(solution)/shard_map/mix_answers/pallas_call | solution.py:159
  228.3 60.1 %all-to-all-done.1 = bf16[128,40,512]{2,1,0:T(8,128)(2,1)} async-done(((bf16[128,40,512]{2,1,0:T(8,128)(2,1)}), bf16[128,40,512]{2,1,0:T(8,128)(2,1)}, u32[]{:S(2)}, u32[]{:S(2)}) %all-to-all-start.1) | async-done | bytes 5242912 | tf_op jit(solution)/shard_map/all_to_all | solution.py:265
  288.4 3.9 %mix_answers.3 = bf16[2,128,2048]{2,1,0:T(8,128)(2,1)} custom-call(s32[2,8,128]{2,1,0:T(8,128)} %bitcast.18, f32[2,8,128]{2,1,0:T(8,128)} %bitcast.20, bf16[128,5,8,512]{3,2,1,0:T(8,128)(2,1)} %bitcast.6.rows_ref, bf16[2,128,2048]{2,1,0:T(8,128)(2,1)} %mix_answers.2.rest_0_), custom_call_target="tpu_custom_call", output_to_operand_aliasing={{}: (3, {})} | custom-call | tf_op jit(solution)/shard_map/mix_answers/pallas_call | solution.py:159
Async XLA Ops:
  4.1 75.7 %all-to-all-start.2 = ((bf16[128,40,512]{2,1,0:T(8,128)(2,1)}), bf16[128,40,512]{2,1,0:T(8,128)(2,1)}, u32[]{:S(2)}, u32[]{:S(2)}) async-start(bf16[128,40,512]{2,1,0:T(8,128)(2,1)} %bitcast.12), calls=%async_computation.2 | async-start | bytes 10485760 | tf_op jit(solution)/shard_map/all_to_all | solution.py:265
  79.8 6.3 %copy-start = (s32[1,3]{1,0:T(1,128)S(1)}, s32[1,3]{1,0:T(1,128)}, u32[]{:S(2)}) copy-start(s32[1,3]{1,0:T(1,128)} %param.12) | copy-start | bytes 40
  79.8 69.6 %all-to-all-start = ((bf16[128,40,512]{2,1,0:T(8,128)(2,1)}), bf16[128,40,512]{2,1,0:T(8,128)(2,1)}, u32[]{:S(2)}, u32[]{:S(2)}) async-start(bf16[128,40,512]{2,1,0:T(8,128)(2,1)} %bitcast.11), calls=%async_computation | async-start | bytes 10485760 | tf_op jit(solution)/shard_map/all_to_all | solution.py:265
  149.4 69.5 %all-to-all-start.3 = ((bf16[128,40,512]{2,1,0:T(8,128)(2,1)}), bf16[128,40,512]{2,1,0:T(8,128)(2,1)}, u32[]{:S(2)}, u32[]{:S(2)}) async-start(bf16[128,40,512]{2,1,0:T(8,128)(2,1)} %bitcast.13), calls=%async_computation.3 | async-start | bytes 10485760 | tf_op jit(solution)/shard_map/all_to_all | solution.py:265
  218.9 69.5 %all-to-all-start.1 = ((bf16[128,40,512]{2,1,0:T(8,128)(2,1)}), bf16[128,40,512]{2,1,0:T(8,128)(2,1)}, u32[]{:S(2)}, u32[]{:S(2)}) async-start(bf16[128,40,512]{2,1,0:T(8,128)(2,1)} %bitcast.14), calls=%async_computation.1 | async-start | bytes 10485760 | tf_op jit(solution)/shard_map/all_to_all | solution.py:265
